TPU v7x, 32 devices: a whole 2x2x4 slice. The times are simulated.
32 devices in a mesh: fsdp: 4 (over y, x), ctx: 2 (over core), tp: 4 (over z).
Axes of the slice: x: 2, y: 2, z: 4, core: 2. Of those that a mesh axis runs over, the one named last changes fastest.
Arguments:
- layer_input: bfloat16 [4, 1024, 768], P('fsdp', 'ctx'), may hold values from -6 to 6
- doc_ids: int32 [4, 1024], P('fsdp'), may hold values from 0 to 2, never falling along the last dimension, each value on 1 to 800 neighbouring positions
- query_weight: bfloat16 [768, 768], P(('fsdp', 'ctx'), 'tp'), may hold values from -0.109375 to 0.109375
- key_weight: bfloat16 [768, 768], P(('fsdp', 'ctx'), 'tp'), may hold values from -0.109375 to 0.109375
- value_weight: bfloat16 [768, 768], P(('fsdp', 'ctx'), 'tp'), may hold values from -0.21875 to 0.21875
- output_weight: bfloat16 [768, 768], P(('fsdp', 'ctx'), 'tp'), may hold values from -0.875 to 0.875
- gate_weight: bfloat16 [768, 2048], P(('fsdp', 'ctx'), 'tp'), may hold values from -0.21875 to 0.21875
- up_weight: bfloat16 [768, 2048], P(('fsdp', 'ctx'), 'tp'), may hold values from -0.21875 to 0.21875
- down_weight: bfloat16 [768, 2048], P(('fsdp', 'ctx'), 'tp'), may hold values from -0.1875 to 0.1875
- first_gain: bfloat16 [768], P(('fsdp', 'ctx')), may hold values from 0.5 to 1.5
- second_gain: bfloat16 [768], P(('fsdp', 'ctx')), may hold values from 0.5 to 1.5
- position_bias: float32 [32, 12], P(None, 'tp'), may hold values from -4 to 4
- cotangent: bfloat16 [4, 1024, 768], P('fsdp', 'ctx'), may hold values from -6 to 6
Outputs:
- layer_output: bfloat16 [4, 1024, 768], P('fsdp', 'ctx')
- input_gradient: float32 [4, 1024, 768], P('fsdp', 'ctx')
- query_gradient: float32 [768, 768], P(('fsdp', 'ctx'), 'tp')
- key_gradient: float32 [768, 768], P(('fsdp', 'ctx'), 'tp')
- value_gradient: float32 [768, 768], P(('fsdp', 'ctx'), 'tp')
- output_gradient: float32 [768, 768], P(('fsdp', 'ctx'), 'tp')
- gate_gradient: float32 [768, 2048], P(('fsdp', 'ctx'), 'tp')
- up_gradient: float32 [768, 2048], P(('fsdp', 'ctx'), 'tp')
- down_gradient: float32 [768, 2048], P(('fsdp', 'ctx'), 'tp')
- first_gain_gradient: float32 [768], P(('fsdp', 'ctx'))
- second_gain_gradient: float32 [768], P(('fsdp', 'ctx'))
- bias_gradient: float32 [32, 12], P(None, 'tp')
Inputs may be any that keep to these rules, and one draw needn't show every extreme that they name: `doc_ids`: along each sequence the numbers never fall; each of 0 to 2 covers 1 to 800 positions of every sequence, and one covers exactly 800.
All inputs are finite; a program needn't handle non-finite values.
Results may differ from a plain program's by a relative error of at most 0.02.
Values may be sent and summed in bfloat16 or wider, within the bound.
A program may use at most 128 MiB of HBM per device.

v0:
```python
import jax
import jax.numpy as jnp
from jax import lax
from jax.sharding import PartitionSpec as P

DH = 64


epsilon = 1e-06
masked_score = -1000000000.0
bucket_edges = (12, 16, 23, 32, 46, 64, 91)
highest = lax.Precision.HIGHEST


def bucket_of(relative):
    distance = jnp.abs(relative)
    beyond = jnp.zeros_like(distance) + 8
    for edge_value in bucket_edges:
        beyond = beyond + (distance >= edge_value).astype(jnp.int32)
    inside = jnp.where(distance < 8, distance, beyond)
    return jnp.where(relative > 0, 16, 0) + inside


def rms_norm(values, gain_vector):
    inverse = lax.rsqrt(jnp.mean(values * values, axis=-1, keepdims=True) + epsilon)
    return values * inverse * gain_vector


def gated_unit(gate_in, up_in):
    return jax.nn.gelu(gate_in, approximate=True) * up_in


def relative_bias(bias_table, query_rows, key_rows, offset):
    span_width = key_rows + query_rows
    relative = lax.iota(jnp.int32, span_width) - (query_rows - 1) - offset
    one_hot = (
        bucket_of(relative)[:, None] == lax.iota(jnp.int32, bias_table.shape[0])[None, :]
    ).astype(jnp.float32)
    per_shift = jnp.dot(one_hot, bias_table, precision=highest).T
    heads_here = bias_table.shape[1]
    toeplitz = jnp.broadcast_to(per_shift[:, None, :], (heads_here, query_rows, span_width))
    toeplitz = toeplitz.reshape(heads_here, query_rows * span_width)[
        :, : query_rows * (span_width - 1)
    ]
    toeplitz = toeplitz.reshape(heads_here, query_rows, span_width - 1)
    return (toeplitz[:, :, query_rows - 1 : query_rows - 1 + key_rows], one_hot)


def diagonal_sums(grad_scores, query_rows, key_rows):
    heads_here = grad_scores.shape[0]
    span_width = key_rows + query_rows
    placed = jnp.pad(grad_scores, ((0, 0), (0, 0), (query_rows - 1, 0)))
    placed = placed.reshape(heads_here, query_rows * (span_width - 1))
    placed = jnp.pad(placed, ((0, 0), (0, query_rows)))
    return jnp.sum(placed.reshape(heads_here, query_rows, span_width), axis=1)


def on_device(
    layer_input,
    doc_ids,
    query_weight,
    key_weight,
    value_weight,
    output_weight,
    gate_weight,
    up_weight,
    down_weight,
    first_gain,
    second_gain,
    position_bias,
    cotangent,
):
    query_rows = layer_input.shape[1]
    key_rows = query_rows * lax.axis_size("ctx")
    heads_here = position_bias.shape[1]
    head_width = heads_here * DH
    offset = lax.axis_index("ctx") * query_rows
    everything = (
        query_weight,
        key_weight,
        value_weight,
        output_weight,
        gate_weight,
        up_weight,
        down_weight,
        first_gain,
        second_gain,
    )
    (
        full_query,
        full_key,
        full_value,
        full_output,
        full_gate,
        full_up,
        full_down,
        gain_one,
        gain_two,
    ) = (
        lax.all_gather(everything[0], ("fsdp", "ctx"), axis=0, tiled=True),
        lax.all_gather(everything[1], ("fsdp", "ctx"), axis=0, tiled=True),
        lax.all_gather(everything[2], ("fsdp", "ctx"), axis=0, tiled=True),
        lax.all_gather(everything[3], ("fsdp", "ctx"), axis=0, tiled=True),
        lax.all_gather(everything[4], ("fsdp", "ctx"), axis=0, tiled=True),
        lax.all_gather(everything[5], ("fsdp", "ctx"), axis=0, tiled=True),
        lax.all_gather(everything[6], ("fsdp", "ctx"), axis=0, tiled=True),
        lax.all_gather(everything[7], ("fsdp", "ctx"), axis=0, tiled=True),
        lax.all_gather(everything[8], ("fsdp", "ctx"), axis=0, tiled=True),
    )
    inputs = layer_input.astype(jnp.float32)
    gain_first = gain_one.astype(jnp.float32)
    gain_second = gain_two.astype(jnp.float32)
    normed_one = rms_norm(inputs, gain_first).astype(jnp.bfloat16)
    queries = jnp.dot(normed_one, full_query, preferred_element_type=jnp.float32).astype(
        jnp.bfloat16
    )
    keys_local = jnp.dot(normed_one, full_key, preferred_element_type=jnp.float32).astype(
        jnp.bfloat16
    )
    values_local = jnp.dot(normed_one, full_value, preferred_element_type=jnp.float32).astype(
        jnp.bfloat16
    )
    keys_all, values_all = (
        lax.all_gather(keys_local, "ctx", axis=1, tiled=True),
        lax.all_gather(values_local, "ctx", axis=1, tiled=True),
    )
    bias_block, one_hot = relative_bias(position_bias, query_rows, key_rows, offset)

    def scores_of(query_heads, key_heads, id_row):
        raw_scores = jnp.einsum(
            "qhd,khd->hqk", query_heads, key_heads, preferred_element_type=jnp.float32
        )
        own_ids = lax.dynamic_slice_in_dim(id_row, offset, query_rows)
        same_doc = own_ids[:, None] == id_row[None, :]
        return jnp.where(same_doc[None], raw_scores + bias_block, masked_score)

    def forward_one(packed):
        query_seq, key_seq, value_seq, id_row = packed
        scores = scores_of(
            query_seq.reshape(query_rows, heads_here, DH),
            key_seq.reshape(key_rows, heads_here, DH),
            id_row,
        )
        row_max = jnp.max(scores, axis=-1, keepdims=True)
        exponentials = jnp.exp(scores - row_max)
        row_total = jnp.sum(exponentials, axis=-1, keepdims=True)
        probabilities = (exponentials / row_total).astype(jnp.bfloat16)
        attended = jnp.einsum(
            "hqk,khd->qhd",
            probabilities,
            value_seq.reshape(key_rows, heads_here, DH),
            preferred_element_type=jnp.float32,
        )
        log_row = row_max[..., 0] + jnp.log(row_total[..., 0])
        return (attended.reshape(query_rows, head_width).astype(jnp.bfloat16), log_row)

    attended, log_sums = lax.map(forward_one, (queries, keys_all, values_all, doc_ids))
    attention_terms = jnp.einsum(
        "sqe,de->sqd", attended, full_output, preferred_element_type=jnp.float32
    )
    residual = inputs + lax.psum(attention_terms.astype(jnp.bfloat16), "tp").astype(jnp.float32)
    normed_two = rms_norm(residual, gain_second).astype(jnp.bfloat16)
    gate_pre = jnp.dot(normed_two, full_gate, preferred_element_type=jnp.float32)
    up_pre = jnp.dot(normed_two, full_up, preferred_element_type=jnp.float32)
    activated = gated_unit(gate_pre, up_pre).astype(jnp.bfloat16)
    ffn_terms = jnp.einsum("sqf,df->sqd", activated, full_down, preferred_element_type=jnp.float32)
    output_rows = (
        residual + lax.psum(ffn_terms.astype(jnp.bfloat16), "tp").astype(jnp.float32)
    ).astype(jnp.bfloat16)
    grad_activated = jnp.einsum(
        "sqd,df->sqf", cotangent, full_down, preferred_element_type=jnp.float32
    )
    down_grad = jnp.einsum("sqd,sqf->df", cotangent, activated, preferred_element_type=jnp.float32)
    gated_value, gated_back = jax.vjp(gated_unit, gate_pre, up_pre)
    grad_gate, grad_up = gated_back(grad_activated)
    grad_gate = grad_gate.astype(jnp.bfloat16)
    grad_up = grad_up.astype(jnp.bfloat16)
    gate_grad = jnp.einsum("sqd,sqf->df", normed_two, grad_gate, preferred_element_type=jnp.float32)
    up_grad = jnp.einsum("sqd,sqf->df", normed_two, grad_up, preferred_element_type=jnp.float32)
    normed_two_terms = jnp.einsum(
        "sqf,df->sqd", grad_gate, full_gate, preferred_element_type=jnp.float32
    ) + jnp.einsum("sqf,df->sqd", grad_up, full_up, preferred_element_type=jnp.float32)
    grad_normed_two = lax.psum(normed_two_terms.astype(jnp.bfloat16), "tp").astype(jnp.float32)
    second_value, second_back = jax.vjp(rms_norm, residual, gain_second)
    grad_residual, second_gain_grad = second_back(grad_normed_two)
    grad_residual = grad_residual + cotangent.astype(jnp.float32)
    grad_low = grad_residual.astype(jnp.bfloat16)
    grad_attended = jnp.einsum(
        "sqd,de->sqe", grad_low, full_output, preferred_element_type=jnp.float32
    ).astype(jnp.bfloat16)
    output_grad = jnp.einsum("sqd,sqe->de", grad_low, attended, preferred_element_type=jnp.float32)

    def backward_one(running, packed):
        query_seq, key_seq, value_seq, id_row, grad_seq, log_row = packed
        query_heads = query_seq.reshape(query_rows, heads_here, DH)
        key_heads = key_seq.reshape(key_rows, heads_here, DH)
        value_heads = value_seq.reshape(key_rows, heads_here, DH)
        grad_heads = grad_seq.reshape(query_rows, heads_here, DH)
        scores = scores_of(query_heads, key_heads, id_row)
        probabilities = jnp.exp(scores - log_row[..., None])
        grad_probs = jnp.einsum(
            "qhd,khd->hqk", grad_heads, value_heads, preferred_element_type=jnp.float32
        )
        grad_values = jnp.einsum(
            "hqk,qhd->khd",
            probabilities.astype(jnp.bfloat16),
            grad_heads,
            preferred_element_type=jnp.float32,
        )
        grad_scores = probabilities * (
            grad_probs - jnp.sum(probabilities * grad_probs, axis=-1, keepdims=True)
        )
        low_scores = grad_scores.astype(jnp.bfloat16)
        grad_queries = jnp.einsum(
            "hqk,khd->qhd", low_scores, key_heads, preferred_element_type=jnp.float32
        )
        grad_keys = jnp.einsum(
            "hqk,qhd->khd", low_scores, query_heads, preferred_element_type=jnp.float32
        )
        running = running + diagonal_sums(grad_scores, query_rows, key_rows)
        return (
            running,
            (
                grad_queries.reshape(query_rows, head_width).astype(jnp.bfloat16),
                grad_keys.reshape(key_rows, head_width),
                grad_values.reshape(key_rows, head_width),
            ),
        )

    shift_grads, (grad_queries, key_parts, value_parts) = lax.scan(
        backward_one,
        jnp.zeros((heads_here, query_rows + key_rows), jnp.float32),
        (queries, keys_all, values_all, doc_ids, grad_attended, log_sums),
    )
    grad_keys, grad_values = (
        lax.psum_scatter(
            key_parts.astype(jnp.bfloat16), "ctx", scatter_dimension=1, tiled=True
        ).astype(jnp.float32),
        lax.psum_scatter(
            value_parts.astype(jnp.bfloat16), "ctx", scatter_dimension=1, tiled=True
        ).astype(jnp.float32),
    )
    grad_keys = grad_keys.astype(jnp.bfloat16)
    grad_values = grad_values.astype(jnp.bfloat16)
    normed_one_terms = (
        jnp.einsum("sqe,de->sqd", grad_queries, full_query, preferred_element_type=jnp.float32)
        + jnp.einsum("sqe,de->sqd", grad_keys, full_key, preferred_element_type=jnp.float32)
        + jnp.einsum("sqe,de->sqd", grad_values, full_value, preferred_element_type=jnp.float32)
    )
    grad_normed_one = lax.psum(normed_one_terms.astype(jnp.bfloat16), "tp").astype(jnp.float32)
    query_grad = jnp.einsum(
        "sqd,sqe->de", normed_one, grad_queries, preferred_element_type=jnp.float32
    )
    key_grad = jnp.einsum("sqd,sqe->de", normed_one, grad_keys, preferred_element_type=jnp.float32)
    value_grad = jnp.einsum(
        "sqd,sqe->de", normed_one, grad_values, preferred_element_type=jnp.float32
    )
    first_value, first_back = jax.vjp(rms_norm, inputs, gain_first)
    grad_inputs, first_gain_grad = first_back(grad_normed_one)
    input_rows = grad_residual + grad_inputs
    bias_gradient = lax.psum(jnp.dot(one_hot.T, shift_grads.T, precision=highest), ("fsdp", "ctx"))
    (
        query_total,
        key_total,
        value_total,
        output_total,
        gate_total,
        up_total,
        down_total,
        first_total,
        second_total,
    ) = (
        lax.psum_scatter(query_grad, ("fsdp", "ctx"), scatter_dimension=0, tiled=True),
        lax.psum_scatter(key_grad, ("fsdp", "ctx"), scatter_dimension=0, tiled=True),
        lax.psum_scatter(value_grad, ("fsdp", "ctx"), scatter_dimension=0, tiled=True),
        lax.psum_scatter(output_grad, ("fsdp", "ctx"), scatter_dimension=0, tiled=True),
        lax.psum_scatter(gate_grad, ("fsdp", "ctx"), scatter_dimension=0, tiled=True),
        lax.psum_scatter(up_grad, ("fsdp", "ctx"), scatter_dimension=0, tiled=True),
        lax.psum_scatter(down_grad, ("fsdp", "ctx"), scatter_dimension=0, tiled=True),
        lax.psum_scatter(first_gain_grad, ("fsdp", "ctx"), scatter_dimension=0, tiled=True),
        lax.psum_scatter(second_gain_grad, ("fsdp", "ctx"), scatter_dimension=0, tiled=True),
    )
    return (
        output_rows,
        input_rows,
        query_total,
        key_total,
        value_total,
        output_total,
        gate_total,
        up_total,
        down_total,
        first_total,
        second_total,
        bias_gradient,
    )


def solution(mesh):
    return jax.shard_map(
        on_device,
        mesh=mesh,
        in_specs=(
            P("fsdp", "ctx", None),
            P("fsdp", None),
            P(("fsdp", "ctx"), "tp"),
            P(("fsdp", "ctx"), "tp"),
            P(("fsdp", "ctx"), "tp"),
            P(("fsdp", "ctx"), "tp"),
            P(("fsdp", "ctx"), "tp"),
            P(("fsdp", "ctx"), "tp"),
            P(("fsdp", "ctx"), "tp"),
            P(("fsdp", "ctx")),
            P(("fsdp", "ctx")),
            P(None, "tp"),
            P("fsdp", "ctx", None),
        ),
        out_specs=(
            P("fsdp", "ctx", None),
            P("fsdp", "ctx", None),
            P(("fsdp", "ctx"), "tp"),
            P(("fsdp", "ctx"), "tp"),
            P(("fsdp", "ctx"), "tp"),
            P(("fsdp", "ctx"), "tp"),
            P(("fsdp", "ctx"), "tp"),
            P(("fsdp", "ctx"), "tp"),
            P(("fsdp", "ctx"), "tp"),
            P(("fsdp", "ctx")),
            P(("fsdp", "ctx")),
            P(None, "tp"),
        ),
        check_vma=False,
    )
```

profile of v0, /device:TPU:0, one launch (start us, length us, event | category | flops | bytes accessed | tf_op | source)
XLA Modules:
  0.0 631.9 jit_solution(5921621748981540029)
XLA Ops:
  7.3 11.3 %all_gather.34 = bf16[768,192]{1,0:T(8,128)(2,1)S(1)} all-gather(bf16[96,192]{1,0:T(8,128)(2,1)} %param.17), channel_id=1, replica_groups=mesh['fsdp'=4,'ctx'=2,'tp'=4] {'fsdp','ctx'}, dimensions={0}, use_global_device_ids=true | all-gather | bytes 331776 | tf_op jit(solution)/shard_map/all_gather | solution.py:102
  22.2 13.2 %all-reduce.7 = (bf16[768]{0:T(1024)(128)(2,1)S(1)}, bf16[768]{0:T(1024)(128)(2,1)S(1)}) all-reduce(bf16[768]{0:T(1024)(128)(2,1)S(1)} %dynamic-update-slice, bf16[768]{0:T(1024)(128)(2,1)S(1)} %dynamic-update-slice.1), channel_id=1, replica_groups=mesh['fsdp'=4,'ctx'=2,'tp'=4] {'fsdp','ctx'}, use_global_device_ids=true, to_apply=%add.2 | all-reduce | flops 1536 | bytes 6144
  39.0 2.1 all-gather
  42.9 20.4 %copy.29 = f32[1,3,512,1536]{3,1,2,0:T(4,128)S(1)} copy(f32[1,3,512,1536]{3,2,1,0:T(8,128)S(1)} %broadcast_bitcast_fusion) | data formatting | bytes 18874368
  63.3 5.9 slice.8
  69.2 13.2 %reshape.388 = f32[2357760]{0:T(1024)} reshape(f32[3,785920]{1,0:T(4,128)} %slice.8) | data formatting | bytes 18862080
  82.3 15.7 %reshape.361 = f32[3,512,1535]{2,1,0:T(8,128)} reshape(f32[2357760]{0:T(1024)} %reshape.388) | data formatting | bytes 18862080 | tf_op jit(solution)/shard_map/reshape | solution.py:45
  98.0 9.6 %all_gather.36 = bf16[768,192]{1,0:T(8,128)(2,1)S(1)} all-gather(bf16[96,192]{1,0:T(8,128)(2,1)S(1)} %copy-done.37), channel_id=1, replica_groups=mesh['fsdp'=4,'ctx'=2,'tp'=4] {'fsdp','ctx'}, dimensions={0}, use_global_device_ids=true | all-gather | bytes 331776 | tf_op jit(solution)/shard_map/all_gather | solution.py:100
  109.0 9.0 %all_gather.37 = bf16[768,192]{1,0:T(8,128)(2,1)S(1)} all-gather(bf16[96,192]{1,0:T(8,128)(2,1)S(1)} %copy-done.38), channel_id=1, replica_groups=mesh['fsdp'=4,'ctx'=2,'tp'=4] {'fsdp','ctx'}, dimensions={0}, use_global_device_ids=true | all-gather | bytes 331776 | tf_op jit(solution)/shard_map/all_gather | solution.py:101
  118.5 2.1 all-gather.1
  120.6 9.3 %all_gather.39 = bf16[768,192]{1,0:T(8,128)(2,1)S(1)} all-gather(bf16[96,192]{1,0:T(8,128)(2,1)S(1)} %copy-done.39), channel_id=1, replica_groups=mesh['fsdp'=4,'ctx'=2,'tp'=4] {'fsdp','ctx'}, dimensions={0}, use_global_device_ids=true | all-gather | bytes 331776 | tf_op jit(solution)/shard_map/all_gather | solution.py:103
  130.3 5.3 fusion.84
  141.4 10.7 %all_gather.41 = bf16[768,512]{1,0:T(8,128)(2,1)} all-gather(bf16[96,512]{1,0:T(8,128)(2,1)S(1)} %copy-done.32), channel_id=1, replica_groups=mesh['fsdp'=4,'ctx'=2,'tp'=4] {'fsdp','ctx'}, dimensions={0}, use_global_device_ids=true | all-gather | bytes 884736 | tf_op jit(solution)/shard_map/all_gather | solution.py:104
  152.1 10.0 %all_gather.42 = bf16[768,512]{1,0:T(8,128)(2,1)S(1)} all-gather(bf16[96,512]{1,0:T(8,128)(2,1)S(1)} %copy-done.33), channel_id=1, replica_groups=mesh['fsdp'=4,'ctx'=2,'tp'=4] {'fsdp','ctx'}, dimensions={0}, use_global_device_ids=true | all-gather | bytes 884736 | tf_op jit(solution)/shard_map/all_gather | solution.py:105
  162.2 10.9 %all_gather.43 = bf16[768,512]{1,0:T(8,128)(2,1)} all-gather(bf16[96,512]{1,0:T(8,128)(2,1)S(1)} %copy-done.34), channel_id=1, replica_groups=mesh['fsdp'=4,'ctx'=2,'tp'=4] {'fsdp','ctx'}, dimensions={0}, use_global_device_ids=true | all-gather | bytes 884736 | tf_op jit(solution)/shard_map/all_gather | solution.py:106
  173.1 12.3 %all-reduce.13.cloned.1.call-done = bf16[1,512,768]{2,1,0:T(8,128)(2,1)} async-done(((bf16[1,512,768]{2,1,0:T(8,128)(2,1)}), bf16[1,512,768]{2,1,0:T(8,128)(2,1)}) %all-reduce.13.cloned.1.call-update) | async-done | bytes 786448 | tf_op jit(solution)/shard_map/psum | solution.py:161
  190.1 2.1 multiply_convert_fusion.1
  194.8 43.0 %all-reduce.15.cloned.1.call-done = bf16[1,512,768]{2,1,0:T(8,128)(2,1)} async-done(((bf16[1,512,768]{2,1,0:T(8,128)(2,1)}), bf16[1,512,768]{2,1,0:T(8,128)(2,1)}) %all-reduce.15.cloned.1.call-update) | async-done | bytes 786448 | tf_op jit(solution)/shard_map/psum | solution.py:183
  237.8 2.6 fusion.13
  240.5 1.8 fusion.15
  243.3 4.1 multiply_reduce_fusion
  248.9 1.9 fusion.27
  251.7 2.8 fusion.23
  254.6 4.8 fusion.30
  259.5 3.9 fusion.33
  265.7 2.7 fusion.62
  268.4 1.7 reduce-scatter.14.cloned.1.call-done
  270.1 3.3 fusion.26
  277.6 3.1 fusion.89
  280.8 3.1 fusion.90
  284.0 3.0 convolution_bitcast_fusion.1
  287.0 3.1 copy.27
  293.2 8.6 %pad.10 = f32[3,512,1535]{2,1,0:T(8,128)} pad(f32[3,512,1024]{2,1,0:T(8,128)} %copy-done.3, f32[]{:T(128)} %constant.38.clone.1), padding=0_0x0_0x511_0 | pad | bytes 15722500 | tf_op jit(solution)/shard_map/while/body/eval_jaxpr/jit(_pad)/pad | solution.py:52
  301.8 15.2 %reshape.390 = f32[2357760]{0:T(1024)} reshape(f32[3,512,1535]{2,1,0:T(8,128)} %pad.10) | data formatting | bytes 18862080
  317.0 13.2 %reshape.368 = f32[3,785920]{1,0:T(4,128)} reshape(f32[2357760]{0:T(1024)} %reshape.390) | data formatting | bytes 18862080 | tf_op jit(solution)/shard_map/while/body/eval_jaxpr/reshape | solution.py:53
  330.2 7.0 %pad.11 = f32[3,786432]{1,0:T(4,128)S(1)} pad(f32[3,785920]{1,0:T(4,128)} %reshape.368, f32[]{:T(128)} %constant.38.clone.1), padding=0_0x0_512 | pad | bytes 18868228 | tf_op jit(solution)/shard_map/while/body/eval_jaxpr/jit(_pad)/pad | solution.py:54
  337.2 2.5 bitcast_reduce_fusion
  341.7 2.5 all-reduce.17.cloned.1.call-done
  344.2 1.9 fusion.14
  346.1 22.9 %all-reduce.6 = (f32[768]{0:T(1024)S(1)}, f32[768]{0:T(1024)S(1)}, f32[32,3]{0,1:T(4,128)}) all-reduce(f32[768]{0:T(1024)S(1)} %get-tuple-element.104, f32[768]{0:T(1024)S(1)} %copy-done.50, f32[32,3]{0,1:T(4,128)S(1)} %fusion.52), channel_id=13, replica_groups=mesh['fsdp'=4,'ctx'=2,'tp'=4] {'fsdp','ctx'}, use_global_device_ids=true, to_apply=%region_21.22.clone | all-reduce | flops 1632 | bytes 13056
  370.2 3.5 fusion.16
  373.7 8.2 %reduce-scatter.16.cloned.1.call-done = f32[96,192]{1,0:T(8,128)} async-done(((f32[768,192]{1,0:T(8,128)}), f32[96,192]{1,0:T(8,128)}) %reduce-scatter.16.cloned.1.call-update) | async-done | bytes 73744 | tf_op jit(solution)/shard_map/reduce_scatter | solution.py:273
  381.9 38.7 %reduce-scatter.22.cloned.1.call-done = f32[96,192]{1,0:T(8,128)} async-done(((f32[768,192]{1,0:T(8,128)}), f32[96,192]{1,0:T(8,128)}) %reduce-scatter.22.cloned.1.call-update) | async-done | bytes 73744 | tf_op jit(solution)/shard_map/reduce_scatter | solution.py:276
  420.6 42.4 %reduce-scatter.24.cloned.1.call-done = f32[96,512]{1,0:T(8,128)} async-done(((f32[768,512]{1,0:T(8,128)}), f32[96,512]{1,0:T(8,128)}) %reduce-scatter.24.cloned.1.call-update) | async-done | bytes 196624 | tf_op jit(solution)/shard_map/reduce_scatter | solution.py:277
  463.0 42.3 %reduce-scatter.26.cloned.1.call-done = f32[96,512]{1,0:T(8,128)} async-done(((f32[768,512]{1,0:T(8,128)}), f32[96,512]{1,0:T(8,128)}) %reduce-scatter.26.cloned.1.call-update) | async-done | bytes 196624 | tf_op jit(solution)/shard_map/reduce_scatter | solution.py:278
  505.3 42.2 %reduce-scatter.28.cloned.1.call-done = f32[96,512]{1,0:T(8,128)} async-done(((f32[768,512]{1,0:T(8,128)}), f32[96,512]{1,0:T(8,128)}) %reduce-scatter.28.cloned.1.call-update) | async-done | bytes 196624
  547.5 38.8 %reduce-scatter.18.cloned.1.call-done = f32[96,192]{1,0:T(8,128)} async-done(((f32[768,192]{1,0:T(8,128)}), f32[96,192]{1,0:T(8,128)}) %reduce-scatter.18.cloned.1.call-update) | async-done | bytes 73744 | tf_op jit(solution)/shard_map/reduce_scatter | solution.py:274
  586.3 38.6 %reduce-scatter.20.cloned.1.call-done = f32[96,192]{1,0:T(8,128)} async-done(((f32[768,192]{1,0:T(8,128)}), f32[96,192]{1,0:T(8,128)}) %reduce-scatter.20.cloned.1.call-update) | async-done | bytes 73744 | tf_op jit(solution)/shard_map/reduce_scatter | solution.py:275
  (178 shorter events, 39.0 us)
Async XLA Ops:
  7.2 33.9 %copy-start = (f32[32,3]{0,1:T(4,128)S(1)}, f32[32,3]{0,1:T(4,128)}, u32[]{:S(2)}) copy-start(f32[32,3]{0,1:T(4,128)} %param.24) | copy-start | bytes 1156
  7.2 178.2 %all-reduce.13.cloned.1.call-start = ((), (), s32[]{:S(2)}) async-start(), calls=%async_computation.9 | async-start | bytes 1572864 | tf_op jit(solution)/shard_map/psum | solution.py:161
  18.5 22.5 %copy-start.18 = (bf16[768,192]{1,0:T(8,128)(2,1)}, bf16[768,192]{1,0:T(8,128)(2,1)S(1)}, u32[]{:S(2)}) copy-start(bf16[768,192]{1,0:T(8,128)(2,1)S(1)} %all_gather.34) | copy-start | bytes 884740
  37.3 80.7 %copy-start.48 = (f32[512]{0:T(512)}, f32[512]{0:T(512)S(1)}, u32[]{:S(2)}) copy-start(f32[512]{0:T(512)S(1)} %fusion.74) | copy-start | bytes 6148
  41.1 96.0 %copy-start.16 = (bf16[1024,192]{0,1:T(8,128)(2,1)}, bf16[1024,192]{0,1:T(8,128)(2,1)S(1)}, u32[]{:S(2)}) copy-start(bf16[1024,192]{0,1:T(8,128)(2,1)S(1)} %all-gather) | copy-start | bytes 1179652
  41.1 1.8 copy-start.52
  82.3 15.7 %copy-start.37 = (bf16[96,192]{1,0:T(8,128)(2,1)S(1)}, bf16[96,192]{1,0:T(8,128)(2,1)}, u32[]{:S(2)}) copy-start(bf16[96,192]{1,0:T(8,128)(2,1)} %param.15) | copy-start | bytes 110596
  82.3 26.1 %copy-start.4 = (bf16[1,512,768]{2,1,0:T(8,128)(2,1)S(1)}, bf16[1,512,768]{2,1,0:T(8,128)(2,1)}, u32[]{:S(2)}) copy-start(bf16[1,512,768]{2,1,0:T(8,128)(2,1)} %param.13) | copy-start | bytes 2359300
  98.0 10.9 %copy-start.38 = (bf16[96,192]{1,0:T(8,128)(2,1)S(1)}, bf16[96,192]{1,0:T(8,128)(2,1)}, u32[]{:S(2)}) copy-start(bf16[96,192]{1,0:T(8,128)(2,1)} %param.16) | copy-start | bytes 110596
  109.0 21.3 %copy-start.28 = (bf16[512,192]{0,1:T(8,128)(2,1)}, bf16[512,192]{0,1:T(8,128)(2,1)S(1)}, u32[]{:S(2)}) copy-start(bf16[512,192]{0,1:T(8,128)(2,1)S(1)} %convolution_convert_fusion.4) | copy-start | bytes 589828
  109.0 11.6 %copy-start.39 = (bf16[96,192]{1,0:T(8,128)(2,1)S(1)}, bf16[96,192]{1,0:T(8,128)(2,1)}, u32[]{:S(2)}) copy-start(bf16[96,192]{1,0:T(8,128)(2,1)} %param.18) | copy-start | bytes 110596
  109.0 20.9 %copy-start.51 = (s32[1,1024]{1,0:T(1,128)S(1)}, s32[1,1024]{1,0:T(1,128)}, u32[]{:S(2)}) copy-start(s32[1,1024]{1,0:T(1,128)} %param.14) | copy-start | bytes 12292
  118.0 2.6 copy-start.20
  129.9 10.0 %copy-start.8 = (bf16[768,192]{1,0:T(8,128)(2,1)}, bf16[768,192]{1,0:T(8,128)(2,1)S(1)}, u32[]{:S(2)}) copy-start(bf16[768,192]{1,0:T(8,128)(2,1)S(1)} %all_gather.39) | copy-start | bytes 884740
  135.6 2.6 copy-start.2
  135.7 2.7 copy-start.35
  137.1 2.9 copy-start.40
  139.9 12.2 %copy-start.33 = (bf16[96,512]{1,0:T(8,128)(2,1)S(1)}, bf16[96,512]{1,0:T(8,128)(2,1)}, u32[]{:S(2)}) copy-start(bf16[96,512]{1,0:T(8,128)(2,1)} %param.20) | copy-start | bytes 294916
  141.3 20.9 %copy-start.34 = (bf16[96,512]{1,0:T(8,128)(2,1)S(1)}, bf16[96,512]{1,0:T(8,128)(2,1)}, u32[]{:S(2)}) copy-start(bf16[96,512]{1,0:T(8,128)(2,1)} %param.21) | copy-start | bytes 294916
  141.3 96.5 %all-reduce.15.cloned.1.call-start = ((), (), s32[]{:S(2)}) async-start(), calls=%async_computation.10 | async-start | bytes 1572864 | tf_op jit(solution)/shard_map/psum | solution.py:183
  186.9 1.7 copy-start.46
  187.0 1.7 copy-start.42
  193.2 44.6 %copy-start.43 = (f32[512]{0:T(512)S(1)}, f32[512]{0:T(512)}, u32[]{:S(2)}) copy-start(f32[512]{0:T(512)} %copy-done.42) | copy-start | bytes 6148
  194.7 45.8 %copy-start.47 = (f32[512]{0:T(512)S(1)}, f32[512]{0:T(512)}, u32[]{:S(2)}) copy-start(f32[512]{0:T(512)} %copy-done.46) | copy-start | bytes 6148
  194.7 71.0 %reduce-scatter.12.cloned.1.call-start = ((), (), s32[]{:S(2)}) async-start(), calls=%async_computation.11 | async-start | bytes 589824 | tf_op jit(solution)/shard_map/reduce_scatter | solution.py:236
  237.8 2.6 copy-start.11
  240.4 1.8 copy-start.9
  242.7 4.6 copy-start.14
  242.8 4.6 slice-start
  243.3 4.4 slice-start.1
  248.9 2.7 copy-start.3
  251.7 18.4 %reduce-scatter.14.cloned.1.call-start = ((), (), s32[]{:S(2)}) async-start(), calls=%async_computation.12 | async-start | bytes 589824 | tf_op jit(solution)/shard_map/reduce_scatter | solution.py:239
  251.7 2.8 copy-start.15
  259.4 84.7 %all-reduce.17.cloned.1.call-start = ((), (), s32[]{:S(2)}) async-start(), calls=%async_computation.20 | async-start | bytes 3145728 | tf_op jit(solution)/shard_map/psum | solution.py:168
  259.5 4.6 copy-start.22
  265.7 4.4 copy-start.19
  273.4 2.4 copy-start.25
  273.4 108.5 %reduce-scatter.16.cloned.1.call-start = ((), (), s32[]{:S(2)}) async-start(), calls=%async_computation.13 | async-start | bytes 884736 | tf_op jit(solution)/shard_map/reduce_scatter | solution.py:273
  275.7 144.9 %reduce-scatter.22.cloned.1.call-start = ((), (), s32[]{:S(2)}) async-start(), calls=%async_computation.16 | async-start | bytes 884736 | tf_op jit(solution)/shard_map/reduce_scatter | solution.py:276
  277.2 185.8 %reduce-scatter.24.cloned.1.call-start = ((), (), s32[]{:S(2)}) async-start(), calls=%async_computation.17 | async-start | bytes 1769472 | tf_op jit(solution)/shard_map/reduce_scatter | solution.py:277
  280.7 224.6 %reduce-scatter.26.cloned.1.call-start = ((), (), s32[]{:S(2)}) async-start(), calls=%async_computation.18 | async-start | bytes 1769472 | tf_op jit(solution)/shard_map/reduce_scatter | solution.py:278
  283.9 263.6 %reduce-scatter.28.cloned.1.call-start = ((), (), s32[]{:S(2)}) async-start(), calls=%async_computation.19 | async-start | bytes 1769472
  290.1 296.2 %reduce-scatter.18.cloned.1.call-start = ((), (), s32[]{:S(2)}) async-start(), calls=%async_computation.14 | async-start | bytes 884736 | tf_op jit(solution)/shard_map/reduce_scatter | solution.py:274
  292.5 332.4 %reduce-scatter.20.cloned.1.call-start = ((), (), s32[]{:S(2)}) async-start(), calls=%async_computation.15 | async-start | bytes 884736 | tf_op jit(solution)/shard_map/reduce_scatter | solution.py:275
  337.2 2.5 copy-start.30
  341.2 4.9 copy-start.50
  341.2 29.0 %copy-start.45 = (f32[512]{0:T(512)S(1)}, f32[512]{0:T(512)}, u32[]{:S(2)}) copy-start(f32[512]{0:T(512)} %copy-done.44) | copy-start | bytes 6148
  370.2 254.7 %copy-start.1 = (f32[32,3]{0,1:T(4,128)S(1)}, f32[32,3]{0,1:T(4,128)}, u32[]{:S(2)}) copy-start(f32[32,3]{0,1:T(4,128)} %param.24) | copy-start | bytes 1156
  (20 other events, 22.8 us)
Sparse Core Ops, SparseCore 0:
  141.4 43.9 all-reduce.12
  194.8 42.9 all-reduce.14
  251.8 7.0 reduce-scatter.11
  261.1 8.9 reduce-scatter.13
  273.5 70.6 all-reduce.16
  347.8 34.0 reduce-scatter.15
  385.6 34.9 reduce-scatter.21
  424.5 38.4 reduce-scatter.23
  466.9 38.4 reduce-scatter.25
  509.0 38.4 reduce-scatter.27
  551.3 34.9 reduce-scatter.17
  589.9 34.9 reduce-scatter.19
where the time goes:
time: 636 us; the launch traced here: 632 us
  waiting for transfers between devices  311 us (49%)
  local copies, waits for them, and re-layouts  116 us (18%)
  blocking collectives  111 us (17%)
  matrix products  57.7 us (9%)
  other arithmetic  18.6 us (3%)
  between operations  16.3 us (3%)
    unnamed x124, local copies, waits for them, and re-layouts  65.9 us
    psum x1, waiting for transfers between devices, on_device(): lax.psum(normed_two_terms.astype(jnp.bfloat16), 'tp').astype(jnp.float32)  43 us
    unnamed x13, waiting for transfers between devices  42.4 us
    reduce_scatter x1, waiting for transfers between devices, on_device(): lax.psum_scatter(gate_grad, ('fsdp', 'ctx'), scatter_dimension=0, tiled=T...  42.4 us
    reduce_scatter x1, waiting for transfers between devices, on_device(): lax.psum_scatter(up_grad, ('fsdp', 'ctx'), scatter_dimension=0, tiled=True)  42.3 us
    reduce_scatter x1, waiting for transfers between devices, on_device(): lax.psum_scatter(key_grad, ('fsdp', 'ctx'), scatter_dimension=0, tiled=True)  38.8 us
    reduce_scatter x1, waiting for transfers between devices, on_device(): lax.psum_scatter(output_grad, ('fsdp', 'ctx'), scatter_dimension=0, tiled...  38.7 us
    reduce_scatter x1, waiting for transfers between devices, on_device(): lax.psum_scatter(value_grad, ('fsdp', 'ctx'), scatter_dimension=0, tiled=...  38.6 us
  transfers between devices with their start and end apart: 12, of which 11 were waited for; matrix products, arithmetic and copies ran while one was open for 14% of the time, Pallas kernels for 0%

commit v1 on v0

--- a/solution.py
+++ b/solution.py
@@ -1,6 +1,10 @@
+import functools
+
 import jax
 import jax.numpy as jnp
 from jax import lax
+from jax.experimental import pallas as pl
+from jax.experimental.pallas import tpu as pltpu
 from jax.sharding import PartitionSpec as P
 
 DH = 64
@@ -296,9 +300,936 @@
     )
 
 
+MESH = pl.DeviceIdType.MESH
+bf16, f32 = jnp.bfloat16, jnp.float32
+BLOCK = 128
+QUERY_BLOCK = 256
+CHUNK = 64
+
+
+def contract(left, right, left_dim, right_dim, precision=None):
+    return lax.dot_general(
+        left,
+        right,
+        (((left_dim,), (right_dim,)), ((), ())),
+        preferred_element_type=f32,
+        precision=precision,
+    )
+
+
+def iota(shape, dim):
+    return lax.broadcasted_iota(jnp.int32, shape, dim)
+
+
+def layer_kernel(
+    shards,
+    x_ref,
+    cot_ref,
+    ids_ref,
+    gains_ref,
+    wq_ref,
+    wk_ref,
+    wv_ref,
+    wo_ref,
+    wg_ref,
+    wu_ref,
+    wd_ref,
+    table_ref,
+    out_ref,
+    gin_ref,
+    gq_ref,
+    gk_ref,
+    gv_ref,
+    go_ref,
+    gg_ref,
+    gu_ref,
+    gd_ref,
+    gains_out_ref,
+    bias_out_ref,
+    wa,
+    wf,
+    gains_all,
+    gain_rows,
+    tiles,
+    masked_bias,
+    score,
+    expo,
+    low_score,
+    snd,
+    part,
+    tot,
+    resid,
+    grad_res,
+    n1,
+    n2,
+    grl,
+    n1t,
+    act,
+    ggate,
+    gup,
+    q_t,
+    k_all,
+    v_all,
+    k_t,
+    v_t,
+    att_t,
+    dos_t,
+    dq_t,
+    linv,
+    delta,
+    dk,
+    dv,
+    near,
+    pick,
+    dkv_send,
+    dkv_recv,
+    dkv,
+    gsa,
+    gsf,
+    ra,
+    rf,
+    sa,
+    sf,
+    ra2,
+    rf2,
+    small,
+    small_all,
+    ag_send,
+    ag_recv,
+    kv_send,
+    kv_recv,
+    s1,
+    r1,
+    s2,
+    r2,
+    dkv_ssem,
+    dkv_rsem,
+    rs_send,
+    rs_recv,
+    rs2_send,
+    rs2_recv,
+    sm_send,
+    sm_recv,
+):
+    groups = shards // 2
+    f, c, t = lax.axis_index("fsdp"), lax.axis_index("ctx"), lax.axis_index("tp")
+    me = f * 2 + c
+    rows, width = x_ref.shape
+    keys = k_all.shape[0]
+    head_width = wq_ref.shape[1]
+    heads = head_width // DH
+    units = wg_ref.shape[1]
+    shard = wq_ref.shape[0]
+    chunks = rows // CHUNK
+    partner = (f, 1 - c, t)
+    outer = jnp.logical_or(t == 0, t == 3)
+    inner = jnp.logical_or(t == 1, t == 2)
+    near_end = jnp.where(t < 2, 1, 2)
+    far_end = jnp.where(t < 2, 0, 3)
+    middle = 3 - t
+
+    def remote(source, target, send_sem, recv_sem, device):
+        return pltpu.make_async_remote_copy(
+            src_ref=source,
+            dst_ref=target,
+            send_sem=send_sem,
+            recv_sem=recv_sem,
+            device_id=device,
+            device_id_type=MESH,
+        )
+
+    barrier = pltpu.get_barrier_semaphore()
+    for k in range(groups):
+        for kc in range(2):
+            if k or kc:
+                pl.semaphore_signal(
+                    barrier, inc=1, device_id=(f ^ k, c ^ kc, t), device_id_type=MESH
+                )
+
+    @pl.when(outer)
+    def _():
+        pl.semaphore_signal(barrier, inc=1, device_id=(f, c, near_end), device_id_type=MESH)
+
+    @pl.when(inner)
+    def _():
+        pl.semaphore_signal(barrier, inc=1, device_id=(f, c, far_end), device_id_type=MESH)
+        pl.semaphore_signal(barrier, inc=1, device_id=(f, c, middle), device_id_type=MESH)
+
+    wa[me, 0] = wq_ref[...]
+    wa[me, 1] = wk_ref[...]
+    wa[me, 2] = wv_ref[...]
+    wa[me, 3] = wo_ref[...]
+    wf[me, 0] = wg_ref[...]
+    wf[me, 1] = wu_ref[...]
+    wf[me, 2] = wd_ref[...]
+    gains_all[me] = gains_ref[...]
+
+    @pl.when(outer)
+    def _():
+        pl.semaphore_wait(barrier, shards)
+
+    @pl.when(inner)
+    def _():
+        pl.semaphore_wait(barrier, shards + 1)
+
+    def piece(g, index):
+        if g == 0:
+            return wa.at[index, 0:3]
+        if g == 1:
+            return wa.at[index, 3:4]
+        if g == 2:
+            return wf.at[index, 0:2]
+        if g == 3:
+            return wf.at[index, 2:3]
+        return gains_all.at[index]
+
+    def gather_out(g, k):
+        view = piece(g, me)
+        return remote(view, view, ag_send.at[g, k - 1], ag_recv.at[g, k - 1], (f ^ k, c, t))
+
+    def gather_over(g, k):
+        view = piece(g, (f ^ k) * 2 + c)
+        slot = groups - 1 + k
+        return remote(view, view, ag_send.at[g, slot], ag_recv.at[g, slot], partner)
+
+    def gather_start(g):
+        for k in range(1, groups):
+            gather_out(g, k).start()
+        gather_over(g, 0).start()
+
+    def gather_relay(g):
+        for k in range(1, groups):
+            gather_out(g, k).wait_recv()
+            gather_over(g, k).start()
+
+    def gather_finish(g):
+        for k in range(groups):
+            gather_over(g, k).wait_recv()
+
+    def gather_drain(g):
+        for k in range(1, groups):
+            gather_out(g, k).wait_send()
+        for k in range(groups):
+            gather_over(g, k).wait_send()
+
+    def span(j):
+        return pl.ds(pl.multiple_of(j * CHUNK, CHUNK), CHUNK)
+
+    def end_copy(a, j):
+        return remote(
+            snd.at[a, span(j)], part.at[a, span(j)], s1.at[a, j], r1.at[a, j], (f, c, near_end)
+        )
+
+    def mid_copy(a, j):
+        return remote(
+            snd.at[a, span(j)], tot.at[a, span(j)], s1.at[a, j], r2.at[a, j], (f, c, middle)
+        )
+
+    def total_copy(a, j):
+        return remote(
+            tot.at[a, span(j)], tot.at[a, span(j)], s2.at[a, j], r2.at[a, j], (f, c, far_end)
+        )
+
+    def put(a, j):
+        @pl.when(outer)
+        def _():
+            end_copy(a, j).start()
+
+    def relay_a(a, j):
+        @pl.when(inner)
+        def _():
+            end_copy(a, j).wait_recv()
+            snd[a, span(j)] = (
+                snd[a, span(j)].astype(f32) + part[a, span(j)].astype(f32)
+            ).astype(bf16)
+            mid_copy(a, j).start()
+
+    def relay_b(a, j):
+        @pl.when(inner)
+        def _():
+            mid_copy(a, j).wait_recv()
+            tot[a, span(j)] = (
+                snd[a, span(j)].astype(f32) + tot[a, span(j)].astype(f32)
+            ).astype(bf16)
+            total_copy(a, j).start()
+
+    def finish(a, j):
+        @pl.when(outer)
+        def _():
+            total_copy(a, j).wait_recv()
+
+    def advance(a, s):
+        @pl.when(s < chunks)
+        def _():
+            relay_a(a, jnp.minimum(s, chunks - 1))
+
+        @pl.when(jnp.logical_and(s >= 2, s - 2 < chunks))
+        def _():
+            relay_b(a, jnp.clip(s - 2, 0, chunks - 1))
+
+    def drain(a):
+        def body(j, carry):
+            @pl.when(outer)
+            def _():
+                end_copy(a, j).wait_send()
+
+            @pl.when(inner)
+            def _():
+                mid_copy(a, j).wait_send()
+                total_copy(a, j).wait_send()
+
+            return carry
+
+        lax.fori_loop(0, chunks, body, 0)
+
+    gather_start(4)
+    gather_start(0)
+
+    half = table_ref.shape[0] // 2
+    far = half - 1
+    row_of, column_of = iota((BLOCK, BLOCK), 0), iota((BLOCK, BLOCK), 1)
+    for h in range(heads):
+        tiles[h, 0] = jnp.full((BLOCK, BLOCK), table_ref[far, h], f32)
+        tiles[h, 4] = jnp.full((BLOCK, BLOCK), table_ref[half + far, h], f32)
+    for d in (-1, 0, 1):
+        bucket = bucket_of(d * BLOCK + row_of - column_of)
+        members = range(half) if d < 0 else range(half, 2 * half) if d > 0 else range(2 * half)
+
+        def per_head(h, carry, bucket=bucket, members=members, d=d):
+            filled = jnp.zeros((BLOCK, BLOCK), f32)
+            for b in members:
+                filled = jnp.where(bucket == b, table_ref[b, h], filled)
+            tiles[h, d + 2] = filled
+            return carry
+
+        lax.fori_loop(0, heads, per_head, 0)
+
+    def bias_rows(kb, carry):
+        key_rows = pl.ds(pl.multiple_of(kb * BLOCK, BLOCK), BLOCK)
+        key_ids = jnp.broadcast_to(ids_ref[0:1, key_rows].astype(f32), (BLOCK, BLOCK)).T
+        for qb in range(rows // BLOCK):
+            start = pl.multiple_of(c * rows + qb * BLOCK, BLOCK)
+            query_ids = ids_ref[0:1, pl.ds(start, BLOCK)].astype(f32)
+            same = key_ids == query_ids
+            d = jnp.clip(kb - c * (rows // BLOCK) - qb, -2, 2) + 2
+            for h in range(heads):
+                masked_bias[h, key_rows, qb * BLOCK : (qb + 1) * BLOCK] = jnp.where(
+                    same, tiles[h, d], masked_score
+                )
+        return carry
+
+    lax.fori_loop(0, keys // BLOCK, bias_rows, 0)
+    near[...] = jnp.zeros_like(near)
+    dk[...] = jnp.zeros_like(dk)
+    dv[...] = jnp.zeros_like(dv)
+    small[...] = jnp.zeros_like(small)
+
+    gather_relay(4)
+    gather_relay(0)
+    for g in (1, 2, 3):
+        gather_start(g)
+    gather_finish(4)
+    spread = jnp.zeros((8, width), f32)
+    for i in range(shards):
+        one_hot = (iota((BLOCK, width), 1) == iota((BLOCK, width), 0) + i * shard).astype(f32)
+        spread = spread + contract(gains_all[i].astype(bf16), one_hot.astype(bf16), 1, 0)
+    gain_rows[...] = spread
+
+    def block_rows(b, size=BLOCK):
+        return pl.ds(pl.multiple_of(b * size, size), size)
+
+    def inverse_rms(values):
+        return lax.rsqrt(jnp.mean(values * values, axis=-1, keepdims=True) + epsilon)
+
+    def norm_one(b, carry):
+        at = block_rows(b)
+        xs = x_ref[at, :].astype(f32)
+        n1[at, :] = (xs * inverse_rms(xs) * gain_rows[0:1, :]).astype(bf16)
+        return carry
+
+    lax.fori_loop(0, rows // BLOCK, norm_one, 0)
+    gather_finish(0)
+
+    def weight(buffer, a):
+        return buffer[:, a].reshape(width, buffer.shape[-1])
+
+    own_keys = pl.ds(pl.multiple_of(c * rows, rows), rows)
+    normed = n1[...]
+    k_all[own_keys, :] = contract(normed, weight(wa, 1), 1, 0).astype(bf16)
+    v_all[own_keys, :] = contract(normed, weight(wa, 2), 1, 0).astype(bf16)
+    kv_copies = [
+        remote(ref.at[own_keys], ref.at[own_keys], kv_send.at[n], kv_recv.at[n], partner)
+        for n, ref in enumerate((k_all, v_all))
+    ]
+    for copy in kv_copies:
+        copy.start()
+    q_t[...] = contract(normed, weight(wa, 0), 1, 0).astype(bf16).T
+    n1t[...] = normed.T
+    gather_relay(1)
+    for copy in kv_copies:
+        copy.wait_recv()
+    k_t[...] = k_all[...].T
+    v_t[...] = v_all[...].T
+    gather_finish(1)
+
+    head_of = iota((head_width, QUERY_BLOCK), 0)
+
+    def head_only(values, h):
+        inside = jnp.logical_and(head_of >= h * DH, head_of < (h + 1) * DH)
+        return jnp.where(inside, values, jnp.zeros_like(values))
+
+    def attend(qb, carry):
+        at = block_rows(qb, QUERY_BLOCK)
+        for h in range(heads):
+            queries = head_only(q_t[:, at], h)
+            top = jnp.full((8, QUERY_BLOCK), -jnp.inf, f32)
+            for kb in range(keys // BLOCK):
+                span_k = slice(kb * BLOCK, (kb + 1) * BLOCK)
+                block = contract(k_all[span_k, :], queries, 1, 0) + masked_bias[h, span_k, at]
+                score[span_k, :] = block
+                top = jnp.maximum(top, jnp.max(block.reshape(BLOCK // 8, 8, QUERY_BLOCK), axis=0))
+            top = jnp.max(top, axis=0, keepdims=True)
+            total = jnp.zeros((8, QUERY_BLOCK), f32)
+            for kb in range(keys // BLOCK):
+                span_k = slice(kb * BLOCK, (kb + 1) * BLOCK)
+                block = jnp.exp(score[span_k, :] - top)
+                expo[h, span_k, at] = block.astype(bf16)
+                total = total + jnp.sum(block.reshape(BLOCK // 8, 8, QUERY_BLOCK), axis=0)
+            inverse = 1.0 / jnp.sum(total, axis=0, keepdims=True)
+            linv[h : h + 1, at] = inverse
+            mixed = contract(v_t[h * DH : (h + 1) * DH, :], expo[h, :, at], 1, 0)
+            att_t[h * DH : (h + 1) * DH, at] = (mixed * inverse).astype(bf16)
+        attended = att_t[:, at].T
+        snd[0, at, :] = contract(attended, weight(wa, 3), 1, 1).astype(bf16)
+        for j in range(QUERY_BLOCK // CHUNK):
+            put(0, qb * (QUERY_BLOCK // CHUNK) + j)
+        return carry
+
+    lax.fori_loop(0, rows // QUERY_BLOCK, attend, 0)
+
+    for g in (2, 3):
+        gather_relay(g)
+    for g in (2, 3):
+        gather_finish(g)
+
+    per_block = BLOCK // CHUNK
+    scale = 0.7978845608028654
+    advance(0, 0)
+    advance(0, 1)
+
+    def feed_forward(b, carry):
+        for j in range(per_block):
+            advance(0, b * per_block + 2 + j)
+        for j in range(per_block):
+            finish(0, b * per_block + j)
+        at = block_rows(b)
+        res = x_ref[at, :].astype(f32) + tot[0, at, :].astype(f32)
+        resid[at, :] = res
+        normed = (res * inverse_rms(res) * gain_rows[1:2, :]).astype(bf16)
+        n2[at, :] = normed
+        gate = contract(normed, weight(wf, 0), 1, 0)
+        up = contract(normed, weight(wf, 1), 1, 0)
+        down = weight(wf, 2)
+        grad_act = contract(cot_ref[at, :], down, 1, 0)
+        square = gate * gate
+        curve = jnp.tanh(scale * (gate + 0.044715 * square * gate))
+        left = 0.5 * (1.0 + curve)
+        value = gate * left
+        slope = left + 0.5 * gate * (1.0 - curve * curve) * scale * (1.0 + 0.134145 * square)
+        low_act = (value * up).astype(bf16)
+        low_gate = (grad_act * up * slope).astype(bf16)
+        low_up = (grad_act * value).astype(bf16)
+        act[at, :] = low_act
+        ggate[at, :] = low_gate
+        gup[at, :] = low_up
+        snd[1, at, :] = (
+            contract(low_gate, weight(wf, 0), 1, 1) + contract(low_up, weight(wf, 1), 1, 1)
+        ).astype(bf16)
+        for j in range(per_block):
+            put(1, b * per_block + j)
+        snd[2, at, :] = contract(low_act, down, 1, 1).astype(bf16)
+        return carry
+
+    lax.fori_loop(0, rows // BLOCK, feed_forward, 0)
+
+    def put_all(a):
+        def body(j, carry):
+            put(a, j)
+            return carry
+
+        lax.fori_loop(0, chunks, body, 0)
+
+    put_all(2)
+
+    def sent(n, which):
+        if n == 0:
+            return gsf.at[:, which]
+        return gsa.at[:, which, 3:4] if n == 1 else gsa.at[:, which, 0:3]
+
+    def landed(n):
+        return rf.at[...] if n == 0 else ra.at[:, 3:4] if n == 1 else ra.at[:, 0:3]
+
+    def over_copy(n):
+        return remote(sent(n, 1 - c), landed(n), rs_send.at[n], rs_recv.at[n], partner)
+
+    def summed(n, index):
+        return sf.at[index] if n == 0 else sa.at[index, 3:4] if n == 1 else sa.at[index, 0:3]
+
+    def arrived(n, k):
+        return rf2.at[k - 1] if n == 0 else ra2.at[k - 1, 3:4] if n == 1 else ra2.at[k - 1, 0:3]
+
+    def out_copy(n, k):
+        return remote(
+            summed(n, f ^ k), arrived(n, k), rs2_send.at[n, k - 1], rs2_recv.at[n, k - 1],
+            (f ^ k, c, t),
+        )
+
+    members_of = {0: (0, 1, 2), 1: (3,), 2: (0, 1, 2)}
+    results = {
+        0: (gg_ref, gu_ref, gd_ref),
+        1: (go_ref,),
+        2: (gq_ref, gk_ref, gv_ref),
+    }
+
+    def reduce_send(n):
+        over_copy(n).wait_recv()
+        own, got, total = (gsf, rf, sf) if n == 0 else (gsa, ra, sa)
+
+        def body(k, carry):
+            index = jnp.bitwise_xor(f, groups - 1 - k)
+            for a in members_of[n]:
+                total[index, a] = (
+                    own[index, c, a].astype(f32) + got[index, a].astype(f32)
+                ).astype(bf16)
+            return carry
+
+        lax.fori_loop(0, groups, body, 0)
+        for k in range(1, groups):
+            out_copy(n, k).start()
+
+    def reduce_finish(n):
+        total, got = (sf, rf2) if n == 0 else (sa, ra2)
+        for k in range(1, groups):
+            out_copy(n, k).wait_recv()
+        for a, result in zip(members_of[n], results[n]):
+            value = total[f, a].astype(f32)
+            for k in range(1, groups):
+                value = value + got[k - 1, a].astype(f32)
+            result[...] = value
+
+    def reduce_drain(n):
+        over_copy(n).wait_send()
+        for k in range(1, groups):
+            out_copy(n, k).wait_send()
+
+    both = 2 * shard
+
+    def wide_columns(i):
+        return pl.ds(pl.multiple_of(i * both, both), both)
+
+    def store_grad(buffer, i, a, value):
+        buffer[i, :, a] = value.astype(bf16).reshape(2, shard, value.shape[-1])
+
+    n2_t = n2[...].T
+    cot_t = cot_ref[...].T
+    for i in range(groups):
+        cut = slice(i * both, (i + 1) * both)
+        store_grad(gsf, i, 0, contract(n2_t[cut], ggate[...], 1, 0))
+        store_grad(gsf, i, 1, contract(n2_t[cut], gup[...], 1, 0))
+        store_grad(gsf, i, 2, contract(cot_t[cut], act[...], 1, 0))
+    over_copy(0).start()
+
+    advance(1, 0)
+    advance(1, 1)
+
+    def residual_back(b, carry):
+        for j in range(per_block):
+            advance(1, b * per_block + 2 + j)
+        for j in range(per_block):
+            finish(1, b * per_block + j)
+        at = block_rows(b)
+        grad_in = tot[1, at, :].astype(f32)
+        res = resid[at, :]
+        inverse = inverse_rms(res)
+        u = res * inverse
+        small[1:2, :] += jnp.sum(grad_in * u, axis=0, keepdims=True)
+        g = grad_in * gain_rows[1:2, :]
+        grad = cot_ref[at, :].astype(f32) + inverse * (
+            g - u * jnp.mean(g * u, axis=-1, keepdims=True)
+        )
+        grad_res[at, :] = grad
+        low_grad = grad.astype(bf16)
+        grl[at, :] = low_grad
+        grad_att = contract(low_grad, weight(wa, 3), 1, 0).astype(bf16)
+        scaled = grad_att.T.astype(f32) * jnp.concatenate(
+            [jnp.broadcast_to(linv[h : h + 1, at], (DH, BLOCK)) for h in range(heads)], axis=0
+        )
+        scaled = scaled.astype(bf16)
+        dos_t[:, at] = scaled
+        delta[0:heads, at] = jnp.sum(
+            (scaled.astype(f32) * att_t[:, at].astype(f32)).reshape(heads, DH, BLOCK), axis=1
+        )
+        return carry
+
+    lax.fori_loop(0, rows // BLOCK, residual_back, 0)
+    reduce_send(0)
+
+    extra = dk.shape[1] - head_width
+    query_blocks = rows // BLOCK
+
+    def attend_back(qb, carry):
+        at = block_rows(qb, QUERY_BLOCK)
+        for h in range(heads):
+            grads = head_only(dos_t[:, at], h)
+            queries = head_only(q_t[:, at], h)
+            flag = iota((extra, QUERY_BLOCK), 0)
+            lane = iota((extra, QUERY_BLOCK), 1)
+            flags = jnp.zeros((extra, QUERY_BLOCK), f32)
+            for j in range(QUERY_BLOCK // BLOCK):
+                hit = jnp.logical_and(
+                    flag == h * query_blocks + qb * (QUERY_BLOCK // BLOCK) + j,
+                    jnp.logical_and(lane >= j * BLOCK, lane < (j + 1) * BLOCK),
+                )
+                flags = jnp.where(hit, 1.0, flags)
+            flagged = jnp.concatenate([queries, flags.astype(bf16)], axis=0)
+            shift = delta[h : h + 1, at]
+            for kb in range(keys // BLOCK):
+                span_k = slice(kb * BLOCK, (kb + 1) * BLOCK)
+                block = contract(v_all[span_k, :], grads, 1, 0)
+                low_score[span_k, :] = (
+                    expo[h, span_k, at].astype(f32) * (block - shift)
+                ).astype(bf16)
+            dv[...] += contract(expo[h, :, at], grads, 1, 1)
+            dk[...] += contract(low_score[...], flagged, 1, 1)
+            dq_t[h * DH : (h + 1) * DH, at] = contract(
+                k_t[h * DH : (h + 1) * DH, :], low_score[...], 1, 0
+            ).astype(bf16)
+            for j in range(QUERY_BLOCK // BLOCK):
+                home = c * query_blocks + qb * (QUERY_BLOCK // BLOCK) + j
+                for d in (-1, 0, 1):
+                    kb = home + d
+                    valid = jnp.logical_and(kb >= 0, kb < keys // BLOCK)
+
+                    @pl.when(valid)
+                    def _():
+                        where_k = jnp.clip(kb, 0, keys // BLOCK - 1)
+                        near[h, d + 1] += low_score[
+                            block_rows(where_k), j * BLOCK : (j + 1) * BLOCK
+                        ].astype(f32)
+
+        return carry
+
+    lax.fori_loop(0, rows // QUERY_BLOCK, attend_back, 0)
+
+    other_keys = pl.ds(pl.multiple_of((1 - c) * rows, rows), rows)
+    dkv_send[0] = dk[other_keys, 0:head_width].astype(bf16)
+    dkv_send[1] = dv[other_keys, :].astype(bf16)
+    dkv_copy = remote(dkv_send.at[...], dkv_recv.at[...], dkv_ssem.at[0], dkv_rsem.at[0], partner)
+    dkv_copy.start()
+    grl_t = grl[...].T
+    for i in range(groups):
+        cut = slice(i * both, (i + 1) * both)
+        store_grad(gsa, i, 3, contract(grl_t[cut], att_t[...], 1, 1))
+    over_copy(1).start()
+    dkv_copy.wait_recv()
+    dkv[0] = (dk[own_keys, 0:head_width] + dkv_recv[0].astype(f32)).astype(bf16)
+    dkv[1] = (dv[own_keys, :] + dkv_recv[1].astype(f32)).astype(bf16)
+
+    def project_back(b, carry):
+        at = block_rows(b)
+        total = contract(dq_t[:, at].T, weight(wa, 0), 1, 1)
+        total = total + contract(dkv[0, at, :], weight(wa, 1), 1, 1)
+        total = total + contract(dkv[1, at, :], weight(wa, 2), 1, 1)
+        snd[3, at, :] = total.astype(bf16)
+        for j in range(per_block):
+            put(3, b * per_block + j)
+        return carry
+
+    lax.fori_loop(0, rows // BLOCK, project_back, 0)
+
+    def advance_all(a):
+        def body(s, carry):
+            advance(a, s)
+            return carry
+
+        lax.fori_loop(0, chunks + 2, body, 0)
+
+    def weights_back(i, carry):
+        cut = n1t[wide_columns(i), :]
+        store_grad(gsa, i, 0, contract(cut, dq_t[...], 1, 1))
+        store_grad(gsa, i, 1, contract(cut, dkv[0], 1, 0))
+        store_grad(gsa, i, 2, contract(cut, dkv[1], 1, 0))
+        return carry
+
+    lax.fori_loop(0, groups, weights_back, 0)
+    over_copy(2).start()
+    reduce_send(1)
+    reduce_send(2)
+
+    advance_all(2)
+
+    def bucket_sums(h, carry):
+        for b in range(2 * half):
+            summed_block = jnp.zeros((8, BLOCK), f32)
+            for d in (-1, 0) if b < half else (0, 1):
+                bucket = bucket_of(d * BLOCK + row_of - column_of)
+                chosen = jnp.where(bucket == b, near[h, d + 1], 0.0)
+                summed_block = summed_block + jnp.sum(
+                    chosen.reshape(BLOCK // 8, 8, BLOCK), axis=0
+                )
+            pick[b : b + 1, :] = jnp.sum(summed_block, axis=0, keepdims=True)
+        sums = contract(jnp.ones((8, BLOCK), f32), pick[...], 1, 1, highest)
+        small[:, 0 : 2 * half] += jnp.where(iota((8, 2 * half), 0) == 2 + h, sums, 0.0)
+        return carry
+
+    lax.fori_loop(0, heads, bucket_sums, 0)
+    tail = dk.shape[1] - BLOCK
+    first_lane = head_width - tail
+    column_sums = dk[:, tail:]
+    block_row = iota((keys, BLOCK), 0)
+    lane = iota((keys, BLOCK), 1)
+    left_sum = jnp.zeros((1, BLOCK), f32)
+    right_sum = jnp.zeros((1, BLOCK), f32)
+    for j in range(query_blocks):
+        mine = jnp.zeros((keys, BLOCK), jnp.bool_)
+        for h in range(heads):
+            mine = jnp.logical_or(mine, lane == first_lane + h * query_blocks + j)
+        home = c * query_blocks + j
+        is_left = jnp.logical_and(mine, block_row < (home - 1) * BLOCK)
+        is_right = jnp.logical_and(mine, block_row >= (home + 2) * BLOCK)
+        left_sum += jnp.sum(jnp.where(is_left, column_sums, 0.0), axis=0, keepdims=True)
+        right_sum += jnp.sum(jnp.where(is_right, column_sums, 0.0), axis=0, keepdims=True)
+    from_lane, to_lane = iota((BLOCK, BLOCK), 0), iota((BLOCK, BLOCK), 1)
+    for h in range(heads):
+        start = first_lane + h * query_blocks
+        inside = jnp.logical_and(from_lane >= start, from_lane < start + query_blocks)
+        left_pick = jnp.logical_and(inside, to_lane == far).astype(f32)
+        right_pick = jnp.logical_and(inside, to_lane == half + far).astype(f32)
+        small[2 + h : 3 + h, 0:BLOCK] += (
+            contract(jnp.broadcast_to(left_sum, (8, BLOCK)), left_pick, 1, 0, highest)
+            + contract(jnp.broadcast_to(right_sum, (8, BLOCK)), right_pick, 1, 0, highest)
+        )[0:1]
+
+    advance_all(3)
+
+    def input_back(b, carry):
+        for j in range(per_block):
+            finish(3, b * per_block + j)
+        at = block_rows(b)
+        grad_in = tot[3, at, :].astype(f32)
+        xs = x_ref[at, :].astype(f32)
+        inverse = inverse_rms(xs)
+        u = xs * inverse
+        small[0:1, :] += jnp.sum(grad_in * u, axis=0, keepdims=True)
+        g = grad_in * gain_rows[0:1, :]
+        gin_ref[at, :] = grad_res[at, :] + inverse * (
+            g - u * jnp.mean(g * u, axis=-1, keepdims=True)
+        )
+        return carry
+
+    lax.fori_loop(0, rows // BLOCK, input_back, 0)
+
+    small_copies = [
+        remote(
+            small.at[...], small_all.at[me], sm_send.at[k * 2 + kc - 1], sm_recv.at[k * 2 + kc - 1],
+            (f ^ k, c ^ kc, t),
+        )
+        for k in range(groups)
+        for kc in range(2)
+        if k or kc
+    ]
+    for copy in small_copies:
+        copy.start()
+
+    def layer_out(b, carry):
+        for j in range(per_block):
+            finish(2, b * per_block + j)
+        at = block_rows(b)
+        out_ref[at, :] = (resid[at, :] + tot[2, at, :].astype(f32)).astype(bf16)
+        return carry
+
+    lax.fori_loop(0, rows // BLOCK, layer_out, 0)
+    for n in range(3):
+        reduce_finish(n)
+    small_all[me] = small[...]
+    for copy in small_copies:
+        copy.wait_recv()
+    total_small = small_all[0]
+    for i in range(1, shards):
+        total_small = total_small + small_all[i]
+    to_own = (iota((width, BLOCK), 0) == iota((width, BLOCK), 1) + me * shard).astype(f32)
+    gains_out_ref[...] = contract(total_small, to_own, 1, 0, highest)
+    bias_out_ref[...] = total_small[:, 0:BLOCK]
+
+    for copy in small_copies:
+        copy.wait_send()
+    for g in range(5):
+        gather_drain(g)
+    for copy in kv_copies:
+        copy.wait_send()
+    dkv_copy.wait_send()
+    for a in range(4):
+        drain(a)
+    for n in range(3):
+        reduce_drain(n)
+
+
+def fused_layer(shards, x, cot, ids, gains, weights, table):
+    rows, width = x.shape
+    shard, head_width = weights[0].shape
+    units = weights[4].shape[1]
+    keys = ids.shape[1]
+    heads = head_width // DH
+    groups = shards // 2
+    chunks = rows // CHUNK
+    padded = head_width + (-head_width) % BLOCK
+    if padded - head_width < heads * (rows // BLOCK):
+        padded += BLOCK
+    vmem, dma = pltpu.VMEM, pltpu.SemaphoreType.DMA
+    out_shape = (
+        jax.ShapeDtypeStruct((rows, width), bf16),
+        jax.ShapeDtypeStruct((rows, width), f32),
+        *[jax.ShapeDtypeStruct((shard, head_width), f32)] * 4,
+        *[jax.ShapeDtypeStruct((shard, units), f32)] * 3,
+        jax.ShapeDtypeStruct((8, BLOCK), f32),
+        jax.ShapeDtypeStruct((8, BLOCK), f32),
+    )
+    in_vmem = pl.BlockSpec(memory_space=pltpu.VMEM)
+    scratch = [
+        vmem((shards, 4, shard, head_width), bf16),
+        vmem((shards, 3, shard, units), bf16),
+        vmem((shards, 8, BLOCK), f32),
+        vmem((8, width), f32),
+        vmem((heads, 5, BLOCK, BLOCK), f32),
+        vmem((heads, keys, rows), f32),
+        vmem((keys, QUERY_BLOCK), f32),
+        vmem((heads, keys, rows), bf16),
+        vmem((keys, QUERY_BLOCK), bf16),
+        vmem((4, rows, width), bf16),
+        vmem((4, rows, width), bf16),
+        vmem((4, rows, width), bf16),
+        vmem((rows, width), f32),
+        vmem((rows, width), f32),
+        vmem((rows, width), bf16),
+        vmem((rows, width), bf16),
+        vmem((rows, width), bf16),
+        vmem((width, rows), bf16),
+        vmem((rows, units), bf16),
+        vmem((rows, units), bf16),
+        vmem((rows, units), bf16),
+        vmem((head_width, rows), bf16),
+        vmem((keys, head_width), bf16),
+        vmem((keys, head_width), bf16),
+        vmem((head_width, keys), bf16),
+        vmem((head_width, keys), bf16),
+        vmem((head_width, rows), bf16),
+        vmem((head_width, rows), bf16),
+        vmem((head_width, rows), bf16),
+        vmem((8, rows), f32),
+        vmem((8, rows), f32),
+        vmem((keys, padded), f32),
+        vmem((keys, head_width), f32),
+        vmem((heads, 3, BLOCK, BLOCK), f32),
+        vmem((table.shape[0], BLOCK), f32),
+        vmem((2, rows, head_width), bf16),
+        vmem((2, rows, head_width), bf16),
+        vmem((2, rows, head_width), bf16),
+        vmem((groups, 2, 4, shard, head_width), bf16),
+        vmem((groups, 2, 3, shard, units), bf16),
+        vmem((groups, 4, shard, head_width), bf16),
+        vmem((groups, 3, shard, units), bf16),
+        vmem((groups, 4, shard, head_width), bf16),
+        vmem((groups, 3, shard, units), bf16),
+        vmem((groups - 1, 4, shard, head_width), bf16),
+        vmem((groups - 1, 3, shard, units), bf16),
+        vmem((8, width), f32),
+        vmem((shards, 8, width), f32),
+        dma((5, 2 * groups)),
+        dma((5, 2 * groups)),
+        dma((2,)),
+        dma((2,)),
+        dma((4, chunks)),
+        dma((4, chunks)),
+        dma((4, chunks)),
+        dma((4, chunks)),
+        dma((1,)),
+        dma((1,)),
+        dma((3,)),
+        dma((3,)),
+        dma((3, groups)),
+        dma((3, groups)),
+        dma((shards,)),
+        dma((shards,)),
+    ]
+    return pl.pallas_call(
+        functools.partial(layer_kernel, shards),
+        out_shape=out_shape,
+        in_specs=[in_vmem] * 11 + [pl.BlockSpec(memory_space=pltpu.SMEM)],
+        out_specs=[in_vmem] * len(out_shape),
+        scratch_shapes=scratch,
+        name="layer",
+        compiler_params=pltpu.CompilerParams(
+            collective_id=0, has_side_effects=True, vmem_limit_bytes=63 << 20
+        ),
+    )(x, cot, ids, gains, *weights, table)
+
+
+def on_device_fused(
+    layer_input,
+    doc_ids,
+    query_weight,
+    key_weight,
+    value_weight,
+    output_weight,
+    gate_weight,
+    up_weight,
+    down_weight,
+    first_gain,
+    second_gain,
+    position_bias,
+    cotangent,
+):
+    shards = lax.axis_size("fsdp") * lax.axis_size("ctx")
+    shard = first_gain.shape[0]
+    heads = position_bias.shape[1]
+    gains = jnp.pad(
+        jnp.stack([first_gain, second_gain]).astype(f32), ((0, 6), (0, BLOCK - shard))
+    )
+    outs = fused_layer(
+        shards,
+        layer_input[0],
+        cotangent[0],
+        doc_ids,
+        gains,
+        (
+            query_weight,
+            key_weight,
+            value_weight,
+            output_weight,
+            gate_weight,
+            up_weight,
+            down_weight,
+        ),
+        position_bias,
+    )
+    gains_out, bias_out = outs[9], outs[10]
+    return (
+        outs[0][None],
+        outs[1][None],
+        *outs[2:9],
+        gains_out[0, :shard],
+        gains_out[1, :shard],
+        bias_out[2 : 2 + heads, : position_bias.shape[0]].T,
+    )
+
+
+def fits_kernel(mesh):
+    return mesh.shape["ctx"] == 2 and mesh.shape["tp"] == 4 and mesh.shape["fsdp"] in (2, 4)
+
+
 def solution(mesh):
     return jax.shard_map(
-        on_device,
+        on_device_fused if fits_kernel(mesh) else on_device,
         mesh=mesh,
         in_specs=(
             P("fsdp", "ctx", None),

time: 636 us -> 152 us (0.24)
  waiting for transfers between devices: 311 us -> 0 us
  Pallas kernels: 0 us -> 138 us
  blocking collectives: 111 us -> 0 us
  local copies, waits for them, and re-layouts: 116 us -> 11.8 us
  matrix products: 57.7 us -> 0 us
  other arithmetic: 18.6 us -> 1.27 us
  between operations: 16.3 us -> 0.7 us
    reduce_scatter x8 -> x0, waiting for transfers between devices: 211 us -> none  [the longest x1 42.4 us: on_device(): lax.psum_scatter(gate_grad, ('fsdp', 'ctx'), scatter_dimension=0, tiled=T...]
    pallas_call x0 -> x1, Pallas kernels: none -> 138 us  [fused_layer(): pl.pallas_call(functools.partial(layer_kernel, shards), out_shape=out_sha...]
    all_gather x9 -> x0, blocking collectives: 75.1 us -> none  [the longest x1 11.3 us: on_device(): lax.all_gather(everything[2], ('fsdp', 'ctx'), axis=0, tiled=True)]
    psum x3 -> x0, waiting for transfers between devices: 57.8 us -> none  [the longest x1 43 us: on_device(): lax.psum(normed_two_terms.astype(jnp.bfloat16), 'tp').astype(jnp.float32)]
    dot_general x29 -> x0, matrix products: 57.7 us -> none  [the longest x1 5.32 us: scores_of(): jnp.einsum('qhd,khd->hqk', query_heads, key_heads, preferred_element_type...]
    unnamed x124 -> x26, local copies, waits for them, and re-layouts: 65.9 us -> 9.2 us
    unnamed x13 -> x0, waiting for transfers between devices: 42.4 us -> none
    unnamed x2 -> x0, blocking collectives: 36.1 us -> none
  transfers between devices with their start and end apart: 12 -> 0, of which waited for: 11 -> 0; matrix products, arithmetic and copies ran while one was open for 14% -> 0% of each run, Pallas kernels for 0% -> 0%
where the time goes in v1:
time: 152 us; the launch traced here: 151 us
  Pallas kernels  138 us (91%)
  local copies, waits for them, and re-layouts  11.8 us (8%)
    pallas_call x1, Pallas kernels, fused_layer(): pl.pallas_call(functools.partial(layer_kernel, shards), out_shape=out_sha...  138 us
    unnamed x26, local copies, waits for them, and re-layouts  9.2 us

profile of v1, /device:TPU:0, one launch (start us, length us, event | category | flops | bytes accessed | tf_op | source)
XLA Modules:
  0.0 151.5 jit_solution(10269659353088580079)
XLA Ops:
  0.6 1.4 copy.25.table_ref
  2.0 1.3 fusion.6.gains_ref
  3.3 137.7 %layer.1 = (bf16[512,768]{1,0:T(8,128)(2,1)}, f32[512,768]{1,0:T(8,128)}, f32[96,192]{1,0:T(8,128)}, f32[96,192]{1,0:T(8,128)}, f32[96,192]{1,0:T(8,128)}, /*ind...) custom-call(bf16[512,768]{1,0:T(8,128)(2,1)} %bitcast.14, ...), custom_call_target="tpu_custom_call" | custom-call | tf_op jit(solution)/shard_map/layer/pallas_call | solution.py:1164
  141.0 0.0 copy-start
  141.0 1.3 slice_bitcast_fusion.1
  142.3 1.3 slice_bitcast_fusion
  143.6 2.1 %copy.35 = bf16[1,512,768]{2,1,0:T(8,128)(2,1)} copy(bf16[1,512,768]{2,1,0:T(8,128)(2,1)} %bitcast.13) | data formatting | bytes 1572864
  145.6 0.0 copy-done
  145.7 0.0 copy-start.7
  145.7 0.0 copy-start.6
  145.7 0.0 copy-start.5
  145.7 0.0 copy-start.4
  145.7 0.0 copy-start.3
  145.7 0.0 copy-start.2
  145.7 1.1 copy.36
  146.8 0.0 copy-done.7
  146.8 0.0 copy-start.1
  146.8 0.6 copy.37
  147.5 0.0 copy-done.6
  147.5 0.6 copy.38
  148.1 0.0 copy-done.5
  148.1 0.6 copy.39
  148.8 0.0 copy-done.4
  148.8 0.6 copy.40
  149.4 0.0 copy-done.3
  149.4 0.7 copy.41
  150.1 0.0 copy-done.2
  150.1 0.7 copy.42
  150.8 0.0 copy-done.1
  150.8 0.7 copy.43
Async XLA Ops:
  141.0 4.7 %copy-start = (f32[512,768]{1,0:T(8,128)S(1)}, f32[512,768]{1,0:T(8,128)}, u32[]{:S(2)}) copy-start(f32[512,768]{1,0:T(8,128)} %get-tuple-element.24) | copy-start | bytes 4718596
  145.7 1.2 copy-start.7
  145.7 1.8 %copy-start.6 = (f32[96,192]{1,0:T(8,128)S(1)}, f32[96,192]{1,0:T(8,128)}, u32[]{:S(2)}) copy-start(f32[96,192]{1,0:T(8,128)} %get-tuple-element.51) | copy-start | bytes 221188
  145.7 2.5 %copy-start.5 = (f32[96,192]{1,0:T(8,128)S(1)}, f32[96,192]{1,0:T(8,128)}, u32[]{:S(2)}) copy-start(f32[96,192]{1,0:T(8,128)} %get-tuple-element.52) | copy-start | bytes 221188
  145.7 3.1 %copy-start.4 = (f32[96,192]{1,0:T(8,128)S(1)}, f32[96,192]{1,0:T(8,128)}, u32[]{:S(2)}) copy-start(f32[96,192]{1,0:T(8,128)} %get-tuple-element.53) | copy-start | bytes 221188
  145.7 3.7 %copy-start.3 = (f32[96,512]{1,0:T(8,128)S(1)}, f32[96,512]{1,0:T(8,128)}, u32[]{:S(2)}) copy-start(f32[96,512]{1,0:T(8,128)} %get-tuple-element.54) | copy-start | bytes 589828
  145.7 4.4 %copy-start.2 = (f32[96,512]{1,0:T(8,128)S(1)}, f32[96,512]{1,0:T(8,128)}, u32[]{:S(2)}) copy-start(f32[96,512]{1,0:T(8,128)} %get-tuple-element.55) | copy-start | bytes 589828
  146.8 3.9 %copy-start.1 = (f32[96,512]{1,0:T(8,128)S(1)}, f32[96,512]{1,0:T(8,128)}, u32[]{:S(2)}) copy-start(f32[96,512]{1,0:T(8,128)} %get-tuple-element.56) | copy-start | bytes 589828

commit v2 on v1

--- a/solution.py
+++ b/solution.py
@@ -305,6 +305,7 @@
 BLOCK = 128
 QUERY_BLOCK = 256
 CHUNK = 64
+LAG = 2
 
 
 def contract(left, right, left_dim, right_dim, precision=None):
@@ -326,7 +327,8 @@
     x_ref,
     cot_ref,
     ids_ref,
-    gains_ref,
+    gain_one_ref,
+    gain_two_ref,
     wq_ref,
     wk_ref,
     wv_ref,
@@ -344,7 +346,8 @@
     gg_ref,
     gu_ref,
     gd_ref,
-    gains_out_ref,
+    gain_one_out_ref,
+    gain_two_out_ref,
     bias_out_ref,
     wa,
     wf,
@@ -462,7 +465,9 @@
     wf[me, 0] = wg_ref[...]
     wf[me, 1] = wu_ref[...]
     wf[me, 2] = wd_ref[...]
-    gains_all[me] = gains_ref[...]
+    gains_all[me] = jnp.zeros((8, BLOCK), f32)
+    gains_all[me, 0:1, 0:shard] = gain_one_ref[...].astype(f32)
+    gains_all[me, 1:2, 0:shard] = gain_two_ref[...].astype(f32)
 
     @pl.when(outer)
     def _():
@@ -558,14 +563,16 @@
         def _():
             total_copy(a, j).wait_recv()
 
-    def advance(a, s):
-        @pl.when(s < chunks)
-        def _():
-            relay_a(a, jnp.minimum(s, chunks - 1))
-
-        @pl.when(jnp.logical_and(s >= 2, s - 2 < chunks))
-        def _():
-            relay_b(a, jnp.clip(s - 2, 0, chunks - 1))
+    def service(step):
+        if isinstance(step, int):
+            behind, ahead = divmod(step - LAG, chunks), divmod(step, chunks)
+        else:
+            behind = (lax.div(step - LAG, chunks), lax.rem(step - LAG, chunks))
+            ahead = (lax.div(step, chunks), lax.rem(step, chunks))
+        if not isinstance(step, int) or LAG <= step:
+            relay_b(*behind)
+        if not isinstance(step, int) or step < 4 * chunks:
+            relay_a(*ahead)
 
     def drain(a):
         def body(j, carry):
@@ -585,12 +592,12 @@
     gather_start(4)
     gather_start(0)
 
-    half = table_ref.shape[0] // 2
+    half = table_ref.shape[1] // 2
     far = half - 1
     row_of, column_of = iota((BLOCK, BLOCK), 0), iota((BLOCK, BLOCK), 1)
     for h in range(heads):
-        tiles[h, 0] = jnp.full((BLOCK, BLOCK), table_ref[far, h], f32)
-        tiles[h, 4] = jnp.full((BLOCK, BLOCK), table_ref[half + far, h], f32)
+        tiles[h, 0] = jnp.full((BLOCK, BLOCK), table_ref[h, far], f32)
+        tiles[h, 4] = jnp.full((BLOCK, BLOCK), table_ref[h, half + far], f32)
     for d in (-1, 0, 1):
         bucket = bucket_of(d * BLOCK + row_of - column_of)
         members = range(half) if d < 0 else range(half, 2 * half) if d > 0 else range(2 * half)
@@ -598,7 +605,7 @@
         def per_head(h, carry, bucket=bucket, members=members, d=d):
             filled = jnp.zeros((BLOCK, BLOCK), f32)
             for b in members:
-                filled = jnp.where(bucket == b, table_ref[b, h], filled)
+                filled = jnp.where(bucket == b, table_ref[h, b], filled)
             tiles[h, d + 2] = filled
             return carry
 
@@ -713,13 +720,14 @@
         gather_finish(g)
 
     per_block = BLOCK // CHUNK
+    blocks = rows // BLOCK
     scale = 0.7978845608028654
-    advance(0, 0)
-    advance(0, 1)
+    for step in range(LAG):
+        service(step)
 
     def feed_forward(b, carry):
         for j in range(per_block):
-            advance(0, b * per_block + 2 + j)
+            service(b * per_block + LAG + j)
         for j in range(per_block):
             finish(0, b * per_block + j)
         at = block_rows(b)
@@ -824,27 +832,17 @@
 
     both = 2 * shard
 
-    def wide_columns(i):
-        return pl.ds(pl.multiple_of(i * both, both), both)
-
     def store_grad(buffer, i, a, value):
         buffer[i, :, a] = value.astype(bf16).reshape(2, shard, value.shape[-1])
 
-    n2_t = n2[...].T
-    cot_t = cot_ref[...].T
-    for i in range(groups):
+    def feed_forward_weights(i):
         cut = slice(i * both, (i + 1) * both)
-        store_grad(gsf, i, 0, contract(n2_t[cut], ggate[...], 1, 0))
-        store_grad(gsf, i, 1, contract(n2_t[cut], gup[...], 1, 0))
-        store_grad(gsf, i, 2, contract(cot_t[cut], act[...], 1, 0))
-    over_copy(0).start()
-
-    advance(1, 0)
-    advance(1, 1)
-
-    def residual_back(b, carry):
-        for j in range(per_block):
-            advance(1, b * per_block + 2 + j)
+        n2_t = n2[:, cut].T
+        store_grad(gsf, i, 0, contract(n2_t, ggate[...], 1, 0))
+        store_grad(gsf, i, 1, contract(n2_t, gup[...], 1, 0))
+        store_grad(gsf, i, 2, contract(cot_ref[:, cut].T, act[...], 1, 0))
+
+    def residual_back(b):
         for j in range(per_block):
             finish(1, b * per_block + j)
         at = block_rows(b)
@@ -869,17 +867,13 @@
         delta[0:heads, at] = jnp.sum(
             (scaled.astype(f32) * att_t[:, at].astype(f32)).reshape(heads, DH, BLOCK), axis=1
         )
-        return carry
-
-    lax.fori_loop(0, rows // BLOCK, residual_back, 0)
-    reduce_send(0)
 
     extra = dk.shape[1] - head_width
     query_blocks = rows // BLOCK
 
-    def attend_back(qb, carry):
+    def attend_back(qb, h):
         at = block_rows(qb, QUERY_BLOCK)
-        for h in range(heads):
+        if True:
             grads = head_only(dos_t[:, at], h)
             queries = head_only(q_t[:, at], h)
             flag = iota((extra, QUERY_BLOCK), 0)
@@ -917,25 +911,41 @@
                             block_rows(where_k), j * BLOCK : (j + 1) * BLOCK
                         ].astype(f32)
 
-        return carry
-
-    lax.fori_loop(0, rows // QUERY_BLOCK, attend_back, 0)
+    served = [blocks * per_block + LAG]
+
+    def serve_to(end):
+        while served[0] < end:
+            service(served[0])
+            served[0] += 1
+
+    weight_parts = list(range(groups))
+    ratio = QUERY_BLOCK // BLOCK
+    for qb in range(rows // QUERY_BLOCK):
+        for b in range(qb * ratio, (qb + 1) * ratio):
+            serve_to(chunks + (b + 1) * per_block + LAG)
+            residual_back(b)
+        for h in range(heads):
+            attend_back(qb, h)
+            if weight_parts:
+                feed_forward_weights(weight_parts.pop(0))
+            if qb + 1 < rows // QUERY_BLOCK or h + 1 < heads:
+                serve_to(served[0] + 1)
+        if qb == 0:
+            while weight_parts:
+                feed_forward_weights(weight_parts.pop(0))
+            over_copy(0).start()
 
     other_keys = pl.ds(pl.multiple_of((1 - c) * rows, rows), rows)
     dkv_send[0] = dk[other_keys, 0:head_width].astype(bf16)
     dkv_send[1] = dv[other_keys, :].astype(bf16)
     dkv_copy = remote(dkv_send.at[...], dkv_recv.at[...], dkv_ssem.at[0], dkv_rsem.at[0], partner)
     dkv_copy.start()
-    grl_t = grl[...].T
-    for i in range(groups):
-        cut = slice(i * both, (i + 1) * both)
-        store_grad(gsa, i, 3, contract(grl_t[cut], att_t[...], 1, 1))
-    over_copy(1).start()
+    reduce_send(0)
     dkv_copy.wait_recv()
     dkv[0] = (dk[own_keys, 0:head_width] + dkv_recv[0].astype(f32)).astype(bf16)
     dkv[1] = (dv[own_keys, :] + dkv_recv[1].astype(f32)).astype(bf16)
 
-    def project_back(b, carry):
+    def project_back(b):
         at = block_rows(b)
         total = contract(dq_t[:, at].T, weight(wa, 0), 1, 1)
         total = total + contract(dkv[0, at, :], weight(wa, 1), 1, 1)
@@ -943,32 +953,35 @@
         snd[3, at, :] = total.astype(bf16)
         for j in range(per_block):
             put(3, b * per_block + j)
-        return carry
-
-    lax.fori_loop(0, rows // BLOCK, project_back, 0)
-
-    def advance_all(a):
-        def body(s, carry):
-            advance(a, s)
-            return carry
-
-        lax.fori_loop(0, chunks + 2, body, 0)
-
-    def weights_back(i, carry):
-        cut = n1t[wide_columns(i), :]
+
+    for b in range(blocks):
+        project_back(b)
+        serve_to(served[0] + 1)
+
+    grl_t = grl[...].T
+    for i in range(groups):
+        cut = slice(i * both, (i + 1) * both)
+        store_grad(gsa, i, 3, contract(grl_t[cut], att_t[...], 1, 1))
+    over_copy(1).start()
+    serve_to(3 * chunks + 1)
+
+    def weights_back(i):
+        cut = n1t[i * both : (i + 1) * both, :]
         store_grad(gsa, i, 0, contract(cut, dq_t[...], 1, 1))
         store_grad(gsa, i, 1, contract(cut, dkv[0], 1, 0))
         store_grad(gsa, i, 2, contract(cut, dkv[1], 1, 0))
-        return carry
-
-    lax.fori_loop(0, groups, weights_back, 0)
+
+    for i in range(groups):
+        weights_back(i)
+        if i % 2:
+            serve_to(served[0] + 1)
     over_copy(2).start()
     reduce_send(1)
+    serve_to(served[0] + 1)
     reduce_send(2)
-
-    advance_all(2)
-
-    def bucket_sums(h, carry):
+    serve_to(served[0] + 1)
+
+    def bucket_sums(h):
         for b in range(2 * half):
             summed_block = jnp.zeros((8, BLOCK), f32)
             for d in (-1, 0) if b < half else (0, 1):
@@ -980,39 +993,36 @@
             pick[b : b + 1, :] = jnp.sum(summed_block, axis=0, keepdims=True)
         sums = contract(jnp.ones((8, BLOCK), f32), pick[...], 1, 1, highest)
         small[:, 0 : 2 * half] += jnp.where(iota((8, 2 * half), 0) == 2 + h, sums, 0.0)
-        return carry
-
-    lax.fori_loop(0, heads, bucket_sums, 0)
-    tail = dk.shape[1] - BLOCK
-    first_lane = head_width - tail
-    column_sums = dk[:, tail:]
-    block_row = iota((keys, BLOCK), 0)
-    lane = iota((keys, BLOCK), 1)
-    left_sum = jnp.zeros((1, BLOCK), f32)
-    right_sum = jnp.zeros((1, BLOCK), f32)
-    for j in range(query_blocks):
-        mine = jnp.zeros((keys, BLOCK), jnp.bool_)
+
+    def far_sums():
+        tail = dk.shape[1] - BLOCK
+        first_lane = head_width - tail
+        column_sums = dk[:, tail:]
+        block_row = iota((keys, BLOCK), 0)
+        lane = iota((keys, BLOCK), 1)
+        left_sum = jnp.zeros((1, BLOCK), f32)
+        right_sum = jnp.zeros((1, BLOCK), f32)
+        for j in range(query_blocks):
+            mine = jnp.zeros((keys, BLOCK), jnp.bool_)
+            for h in range(heads):
+                mine = jnp.logical_or(mine, lane == first_lane + h * query_blocks + j)
+            home = c * query_blocks + j
+            is_left = jnp.logical_and(mine, block_row < (home - 1) * BLOCK)
+            is_right = jnp.logical_and(mine, block_row >= (home + 2) * BLOCK)
+            left_sum += jnp.sum(jnp.where(is_left, column_sums, 0.0), axis=0, keepdims=True)
+            right_sum += jnp.sum(jnp.where(is_right, column_sums, 0.0), axis=0, keepdims=True)
+        from_lane, to_lane = iota((BLOCK, BLOCK), 0), iota((BLOCK, BLOCK), 1)
         for h in range(heads):
-            mine = jnp.logical_or(mine, lane == first_lane + h * query_blocks + j)
-        home = c * query_blocks + j
-        is_left = jnp.logical_and(mine, block_row < (home - 1) * BLOCK)
-        is_right = jnp.logical_and(mine, block_row >= (home + 2) * BLOCK)
-        left_sum += jnp.sum(jnp.where(is_left, column_sums, 0.0), axis=0, keepdims=True)
-        right_sum += jnp.sum(jnp.where(is_right, column_sums, 0.0), axis=0, keepdims=True)
-    from_lane, to_lane = iota((BLOCK, BLOCK), 0), iota((BLOCK, BLOCK), 1)
-    for h in range(heads):
-        start = first_lane + h * query_blocks
-        inside = jnp.logical_and(from_lane >= start, from_lane < start + query_blocks)
-        left_pick = jnp.logical_and(inside, to_lane == far).astype(f32)
-        right_pick = jnp.logical_and(inside, to_lane == half + far).astype(f32)
-        small[2 + h : 3 + h, 0:BLOCK] += (
-            contract(jnp.broadcast_to(left_sum, (8, BLOCK)), left_pick, 1, 0, highest)
-            + contract(jnp.broadcast_to(right_sum, (8, BLOCK)), right_pick, 1, 0, highest)
-        )[0:1]
-
-    advance_all(3)
-
-    def input_back(b, carry):
+            start = first_lane + h * query_blocks
+            inside = jnp.logical_and(from_lane >= start, from_lane < start + query_blocks)
+            left_pick = jnp.logical_and(inside, to_lane == far).astype(f32)
+            right_pick = jnp.logical_and(inside, to_lane == half + far).astype(f32)
+            small[2 + h : 3 + h, 0:BLOCK] += (
+                contract(jnp.broadcast_to(left_sum, (8, BLOCK)), left_pick, 1, 0, highest)
+                + contract(jnp.broadcast_to(right_sum, (8, BLOCK)), right_pick, 1, 0, highest)
+            )[0:1]
+
+    def input_back(b):
         for j in range(per_block):
             finish(3, b * per_block + j)
         at = block_rows(b)
@@ -1025,9 +1035,25 @@
         gin_ref[at, :] = grad_res[at, :] + inverse * (
             g - u * jnp.mean(g * u, axis=-1, keepdims=True)
         )
-        return carry
-
-    lax.fori_loop(0, rows // BLOCK, input_back, 0)
+
+    def layer_out(b):
+        for j in range(per_block):
+            finish(2, b * per_block + j)
+        at = block_rows(b)
+        out_ref[at, :] = (resid[at, :] + tot[2, at, :].astype(f32)).astype(bf16)
+
+    fillers = [functools.partial(bucket_sums, h) for h in range(heads)] + [far_sums]
+    fillers += [functools.partial(layer_out, b) for b in range(blocks)]
+    fillers += [functools.partial(reduce_finish, n) for n in range(2)]
+    for b in range(blocks):
+        need = 3 * chunks + (b + 1) * per_block + LAG
+        while served[0] < need:
+            serve_to(served[0] + 1)
+            if fillers and served[0] < need:
+                fillers.pop(0)()
+        input_back(b)
+        if fillers and b + 1 < blocks:
+            fillers.pop(0)()
 
     small_copies = [
         remote(
@@ -1041,16 +1067,9 @@
     for copy in small_copies:
         copy.start()
 
-    def layer_out(b, carry):
-        for j in range(per_block):
-            finish(2, b * per_block + j)
-        at = block_rows(b)
-        out_ref[at, :] = (resid[at, :] + tot[2, at, :].astype(f32)).astype(bf16)
-        return carry
-
-    lax.fori_loop(0, rows // BLOCK, layer_out, 0)
-    for n in range(3):
-        reduce_finish(n)
+    while fillers:
+        fillers.pop(0)()
+    reduce_finish(2)
     small_all[me] = small[...]
     for copy in small_copies:
         copy.wait_recv()
@@ -1058,8 +1077,10 @@
     for i in range(1, shards):
         total_small = total_small + small_all[i]
     to_own = (iota((width, BLOCK), 0) == iota((width, BLOCK), 1) + me * shard).astype(f32)
-    gains_out_ref[...] = contract(total_small, to_own, 1, 0, highest)
-    bias_out_ref[...] = total_small[:, 0:BLOCK]
+    own_gains = contract(total_small, to_own, 1, 0, highest)
+    gain_one_out_ref[...] = own_gains[0:1, 0:shard]
+    gain_two_out_ref[...] = own_gains[1:2, 0:shard]
+    bias_out_ref[...] = total_small[2 : 2 + heads, 0 : 2 * half]
 
     for copy in small_copies:
         copy.wait_send()
@@ -1074,7 +1095,7 @@
         reduce_drain(n)
 
 
-def fused_layer(shards, x, cot, ids, gains, weights, table):
+def fused_layer(shards, x, cot, ids, gain_one, gain_two, weights, table):
     rows, width = x.shape
     shard, head_width = weights[0].shape
     units = weights[4].shape[1]
@@ -1091,8 +1112,9 @@
         jax.ShapeDtypeStruct((rows, width), f32),
         *[jax.ShapeDtypeStruct((shard, head_width), f32)] * 4,
         *[jax.ShapeDtypeStruct((shard, units), f32)] * 3,
-        jax.ShapeDtypeStruct((8, BLOCK), f32),
-        jax.ShapeDtypeStruct((8, BLOCK), f32),
+        jax.ShapeDtypeStruct((1, shard), f32),
+        jax.ShapeDtypeStruct((1, shard), f32),
+        jax.ShapeDtypeStruct(table.shape, f32),
     )
     in_vmem = pl.BlockSpec(memory_space=pltpu.VMEM)
     scratch = [
@@ -1130,7 +1152,7 @@
         vmem((keys, padded), f32),
         vmem((keys, head_width), f32),
         vmem((heads, 3, BLOCK, BLOCK), f32),
-        vmem((table.shape[0], BLOCK), f32),
+        vmem((table.shape[1], BLOCK), f32),
         vmem((2, rows, head_width), bf16),
         vmem((2, rows, head_width), bf16),
         vmem((2, rows, head_width), bf16),
@@ -1164,14 +1186,46 @@
     return pl.pallas_call(
         functools.partial(layer_kernel, shards),
         out_shape=out_shape,
-        in_specs=[in_vmem] * 11 + [pl.BlockSpec(memory_space=pltpu.SMEM)],
+        in_specs=[in_vmem] * 12 + [pl.BlockSpec(memory_space=pltpu.SMEM)],
         out_specs=[in_vmem] * len(out_shape),
         scratch_shapes=scratch,
         name="layer",
         compiler_params=pltpu.CompilerParams(
             collective_id=0, has_side_effects=True, vmem_limit_bytes=63 << 20
         ),
-    )(x, cot, ids, gains, *weights, table)
+    )(x, cot, ids, gain_one, gain_two, *weights, table)
+
+
+def publish_kernel(count, *refs):
+    sources, targets = refs[:count], refs[count : 2 * count]
+    held, in_sem, out_sem = refs[2 * count : 3 * count], refs[3 * count], refs[3 * count + 1]
+    inward = [
+        pltpu.make_async_copy(sources[i], held[i], in_sem.at[i]) for i in range(count)
+    ]
+    outward = [
+        pltpu.make_async_copy(held[i], targets[i], out_sem.at[i]) for i in range(count)
+    ]
+    for copy in inward:
+        copy.start()
+    for arriving, leaving in zip(inward, outward):
+        arriving.wait()
+        leaving.start()
+    for copy in outward:
+        copy.wait()
+
+
+def publish(values):
+    count = len(values)
+    anywhere = pl.BlockSpec(memory_space=pl.ANY)
+    return pl.pallas_call(
+        functools.partial(publish_kernel, count),
+        out_shape=[jax.ShapeDtypeStruct(value.shape, value.dtype) for value in values],
+        in_specs=[anywhere] * count,
+        out_specs=[anywhere] * count,
+        scratch_shapes=[pltpu.VMEM(value.shape, value.dtype) for value in values]
+        + [pltpu.SemaphoreType.DMA((count,))] * 2,
+        name="publish",
+    )(*values)
 
 
 def on_device_fused(
@@ -1190,17 +1244,13 @@
     cotangent,
 ):
     shards = lax.axis_size("fsdp") * lax.axis_size("ctx")
-    shard = first_gain.shape[0]
-    heads = position_bias.shape[1]
-    gains = jnp.pad(
-        jnp.stack([first_gain, second_gain]).astype(f32), ((0, 6), (0, BLOCK - shard))
-    )
     outs = fused_layer(
         shards,
         layer_input[0],
         cotangent[0],
         doc_ids,
-        gains,
+        first_gain[None],
+        second_gain[None],
         (
             query_weight,
             key_weight,
@@ -1210,16 +1260,16 @@
             up_weight,
             down_weight,
         ),
-        position_bias,
-    )
-    gains_out, bias_out = outs[9], outs[10]
+        position_bias.T,
+    )
+    outs = publish(outs)
     return (
         outs[0][None],
         outs[1][None],
         *outs[2:9],
-        gains_out[0, :shard],
-        gains_out[1, :shard],
-        bias_out[2 : 2 + heads, : position_bias.shape[0]].T,
+        outs[9][0],
+        outs[10][0],
+        outs[11].T,
     )
 
 

time: 152 us -> 122 us (0.80)
  Pallas kernels: 138 us -> 121 us
  local copies, waits for them, and re-layouts: 11.8 us -> 0 us
    pallas_call x1, Pallas kernels: 138 us -> 117 us  [fused_layer(): pl.pallas_call(functools.partial(layer_kernel, shards), out_shape=out_sha...]
    unnamed x26 -> x0, local copies, waits for them, and re-layouts: 9.2 us -> none
    pallas_call x0 -> x1, Pallas kernels: none -> 3.33 us  [publish(): pl.pallas_call(functools.partial(publish_kernel, count), out_shape=[jax.S...]
where the time goes in v2:
time: 122 us; the launch traced here: 121 us
  Pallas kernels  121 us (99%)
    pallas_call x1, Pallas kernels, fused_layer(): pl.pallas_call(functools.partial(layer_kernel, shards), out_shape=out_sha...  117 us
    pallas_call x1, Pallas kernels, publish(): pl.pallas_call(functools.partial(publish_kernel, count), out_shape=[jax.S...  3.33 us

profile of v2, /device:TPU:0, one launch (start us, length us, event | category | flops | bytes accessed | tf_op | source)
XLA Modules:
  0.0 121.4 jit_solution(9646426529938476000)
XLA Ops:
  0.6 117.3 %layer.1 = (bf16[512,768]{1,0:T(8,128)(2,1)}, f32[512,768]{1,0:T(8,128)}, f32[96,192]{1,0:T(8,128)}, f32[96,192]{1,0:T(8,128)}, f32[96,192]{1,0:T(8,128)}, /*ind...) custom-call(bf16[512,768]{1,0:T(8,128)(2,1)} %bitcast.10, ...), custom_call_target="tpu_custom_call" | custom-call | tf_op jit(solution)/shard_map/layer/pallas_call | solution.py:1186
  117.9 3.3 %publish.1 = (bf16[512,768]{1,0:T(8,128)(2,1)}, f32[512,768]{1,0:T(8,128)}, f32[96,192]{1,0:T(8,128)}, f32[96,192]{1,0:T(8,128)}, f32[96,192]{1,0:T(8,128)}, /*i...) custom-call(bf16[512,768]{1,0:T(8,128)(2,1)} %get-tuple-element.36.r, ...), custom_call_target="tpu_custom_call" | custom-call | tf_op jit(solution)/shard_map/publish/pallas_call | solution.py:1220

commit v3 on v2

--- a/solution.py
+++ b/solution.py
@@ -304,8 +304,11 @@
 bf16, f32 = jnp.bfloat16, jnp.float32
 BLOCK = 128
 QUERY_BLOCK = 256
-CHUNK = 64
-LAG = 2
+FORWARD_BLOCK = 256
+CHUNK = 32
+LAG = 4
+RELAY_ROWS = 16
+LATE_BLOCK = 1
 
 
 def contract(left, right, left_dim, right_dim, precision=None):
@@ -324,8 +327,8 @@
 
 def layer_kernel(
     shards,
-    x_ref,
-    cot_ref,
+    x_hbm,
+    cot_hbm,
     ids_ref,
     gain_one_ref,
     gain_two_ref,
@@ -337,19 +340,30 @@
     wu_ref,
     wd_ref,
     table_ref,
-    out_ref,
-    gin_ref,
-    gq_ref,
-    gk_ref,
-    gv_ref,
-    go_ref,
-    gg_ref,
-    gu_ref,
-    gd_ref,
+    out_hbm,
+    gin_hbm,
+    gq_hbm,
+    gk_hbm,
+    gv_hbm,
+    go_hbm,
+    gg_hbm,
+    gu_hbm,
+    gd_hbm,
     gain_one_out_ref,
     gain_two_out_ref,
     bias_out_ref,
-    wa,
+    x_ref,
+    cot_ref,
+    out_ref,
+    gin_ref,
+    ga_ref,
+    gf_ref,
+    staged,
+    wkv,
+    wqo,
+    wo3,
+    other_out,
+    wo_all,
     wf,
     gains_all,
     gain_rows,
@@ -367,6 +381,7 @@
     n2,
     grl,
     n1t,
+    turned,
     act,
     ggate,
     gup,
@@ -375,7 +390,7 @@
     v_all,
     k_t,
     v_t,
-    att_t,
+    att_all,
     dos_t,
     dq_t,
     linv,
@@ -397,8 +412,15 @@
     rf2,
     small,
     small_all,
+    gain_part,
+    load_sem,
+    store_sem,
     ag_send,
     ag_recv,
+    zo_send,
+    zo_recv,
+    at_send,
+    at_recv,
     kv_send,
     kv_recv,
     s1,
@@ -413,6 +435,8 @@
     rs2_recv,
     sm_send,
     sm_recv,
+    gp_send,
+    gp_recv,
 ):
     groups = shards // 2
     f, c, t = lax.axis_index("fsdp"), lax.axis_index("ctx"), lax.axis_index("tp")
@@ -424,6 +448,7 @@
     units = wg_ref.shape[1]
     shard = wq_ref.shape[0]
     chunks = rows // CHUNK
+    per_block = BLOCK // CHUNK
     partner = (f, 1 - c, t)
     outer = jnp.logical_or(t == 0, t == 3)
     inner = jnp.logical_or(t == 1, t == 2)
@@ -449,75 +474,97 @@
                     barrier, inc=1, device_id=(f ^ k, c ^ kc, t), device_id_type=MESH
                 )
 
-    @pl.when(outer)
-    def _():
-        pl.semaphore_signal(barrier, inc=1, device_id=(f, c, near_end), device_id_type=MESH)
-
-    @pl.when(inner)
-    def _():
-        pl.semaphore_signal(barrier, inc=1, device_id=(f, c, far_end), device_id_type=MESH)
-        pl.semaphore_signal(barrier, inc=1, device_id=(f, c, middle), device_id_type=MESH)
-
-    wa[me, 0] = wq_ref[...]
-    wa[me, 1] = wk_ref[...]
-    wa[me, 2] = wv_ref[...]
-    wa[me, 3] = wo_ref[...]
-    wf[me, 0] = wg_ref[...]
-    wf[me, 1] = wu_ref[...]
-    wf[me, 2] = wd_ref[...]
+    for kt in range(1, 4):
+        pl.semaphore_signal(
+            barrier, inc=1, device_id=(f, c, t ^ kt), device_id_type=MESH
+        )
+    loads = [
+        pltpu.make_async_copy(source, target, load_sem.at[n])
+        for n, (source, target) in enumerate(
+            (
+                (wk_ref, staged.at[0]),
+                (wv_ref, staged.at[1]),
+                (wq_ref, staged.at[2]),
+                (wo_ref, staged.at[3]),
+                (x_hbm, x_ref),
+                (wg_ref, wf.at[me, 0]),
+                (wu_ref, wf.at[me, 1]),
+                (wd_ref, wf.at[me, 2]),
+                (cot_hbm, cot_ref),
+            )
+        )
+    ]
+    for copy in loads:
+        copy.start()
     gains_all[me] = jnp.zeros((8, BLOCK), f32)
     gains_all[me, 0:1, 0:shard] = gain_one_ref[...].astype(f32)
     gains_all[me, 1:2, 0:shard] = gain_two_ref[...].astype(f32)
-
-    @pl.when(outer)
-    def _():
-        pl.semaphore_wait(barrier, shards)
-
-    @pl.when(inner)
-    def _():
-        pl.semaphore_wait(barrier, shards + 1)
+    for copy in loads[:4]:
+        copy.wait()
+    wkv[me, :, 0:head_width] = staged[0]
+    wkv[me, :, head_width:] = staged[1]
+    wqo[me, :, 0:head_width] = staged[2]
+    wqo[me, :, head_width:] = staged[3]
+    pl.semaphore_wait(barrier, shards - 1 + 3)
 
     def piece(g, index):
-        if g == 0:
-            return wa.at[index, 0:3]
-        if g == 1:
-            return wa.at[index, 3:4]
-        if g == 2:
-            return wf.at[index, 0:2]
-        if g == 3:
-            return wf.at[index, 2:3]
-        return gains_all.at[index]
-
-    def gather_out(g, k):
+        if g < 2:
+            return (wkv, wqo)[g].at[index]
+        return wo3.at[index] if g == 5 else wf.at[index, g - 2]
+
+    def half_piece(g, index, n):
+        return piece(g, index).at[n * (shard // 2) : (n + 1) * (shard // 2)]
+
+    def own_copy(g, k):
         view = piece(g, me)
         return remote(view, view, ag_send.at[g, k - 1], ag_recv.at[g, k - 1], (f ^ k, c, t))
 
-    def gather_over(g, k):
+    def pass_copy(g, k):
+        view = half_piece(g, (f ^ k) * 2 + c, k - 1)
+        return remote(view, view, ag_send.at[g, k + 1], ag_recv.at[g, k + 1], (f ^ (3 - k), c, t))
+
+    def over_piece(g, k):
         view = piece(g, (f ^ k) * 2 + c)
-        slot = groups - 1 + k
-        return remote(view, view, ag_send.at[g, slot], ag_recv.at[g, slot], partner)
-
-    def gather_start(g):
-        for k in range(1, groups):
-            gather_out(g, k).start()
-        gather_over(g, 0).start()
-
-    def gather_relay(g):
-        for k in range(1, groups):
-            gather_out(g, k).wait_recv()
-            gather_over(g, k).start()
+        return remote(view, view, ag_send.at[g, 4 + k], ag_recv.at[g, 4 + k], partner)
+
+    def gather_own(g):
+        for k in (1, 2):
+            own_copy(g, k).start()
+        over_piece(g, 0).start()
+
+    def gather_pass(g):
+        for k in (1, 2):
+            own_copy(g, k).wait_recv()
+            pass_copy(g, k).start()
+            over_piece(g, k).start()
+
+    def gather_corner(g):
+        for k in (1, 2):
+            pass_copy(g, k).wait_recv()
+        over_piece(g, 3).start()
 
     def gather_finish(g):
-        for k in range(groups):
-            gather_over(g, k).wait_recv()
+        for k in range(4):
+            over_piece(g, k).wait_recv()
 
     def gather_drain(g):
-        for k in range(1, groups):
-            gather_out(g, k).wait_send()
-        for k in range(groups):
-            gather_over(g, k).wait_send()
+        for k in (1, 2):
+            own_copy(g, k).wait_send()
+            pass_copy(g, k).wait_send()
+        for k in range(4):
+            over_piece(g, k).wait_send()
+
+    def gain_copy(k):
+        view = gains_all.at[me]
+        return remote(view, view, ag_send.at[6, k], ag_recv.at[6, k], (f ^ k, c, t))
+
+    def gain_over(k):
+        view = gains_all.at[(f ^ k) * 2 + c]
+        return remote(view, view, ag_send.at[6, 4 + k], ag_recv.at[6, 4 + k], partner)
 
     def span(j):
+        if isinstance(j, int):
+            return pl.ds(j * CHUNK, CHUNK)
         return pl.ds(pl.multiple_of(j * CHUNK, CHUNK), CHUNK)
 
     def end_copy(a, j):
@@ -535,47 +582,61 @@
             tot.at[a, span(j)], tot.at[a, span(j)], s2.at[a, j], r2.at[a, j], (f, c, far_end)
         )
 
-    def put(a, j):
+    def add_rows(target, a, j, left, right):
+        def body(r, carry):
+            at = pl.ds(pl.multiple_of(j * CHUNK + r * RELAY_ROWS, RELAY_ROWS), RELAY_ROWS)
+            target[a, at] = (left[a, at].astype(f32) + right[a, at].astype(f32)).astype(bf16)
+            return carry
+
+        lax.fori_loop(0, CHUNK // RELAY_ROWS, body, 0)
+
+    def service(step):
+        def total_step():
+            a, j = split(step - LAG)
+            mid_copy(a, j).wait_recv()
+            add_rows(tot, a, j, snd, tot)
+            total_copy(a, j).start()
+
+        def middle_step():
+            a, j = split(step)
+            end_copy(a, j).wait_recv()
+            add_rows(snd, a, j, snd, part)
+            mid_copy(a, j).start()
+
+        def split(n):
+            if isinstance(n, int):
+                return divmod(n, chunks)
+            return lax.div(n, chunks), lax.rem(n, chunks)
+
+        if isinstance(step, int):
+            if step >= LAG:
+                pl.when(inner)(total_step)
+            if step < 3 * chunks:
+                pl.when(inner)(middle_step)
+        else:
+            pl.when(jnp.logical_and(inner, step >= LAG))(total_step)
+            pl.when(jnp.logical_and(inner, step < 3 * chunks))(middle_step)
+
+    def serve(start, count):
+        for n in range(count):
+            service(start + n)
+
+    def put_block(a, b):
         @pl.when(outer)
         def _():
-            end_copy(a, j).start()
-
-    def relay_a(a, j):
-        @pl.when(inner)
-        def _():
-            end_copy(a, j).wait_recv()
-            snd[a, span(j)] = (
-                snd[a, span(j)].astype(f32) + part[a, span(j)].astype(f32)
-            ).astype(bf16)
-            mid_copy(a, j).start()
-
-    def relay_b(a, j):
-        @pl.when(inner)
-        def _():
-            mid_copy(a, j).wait_recv()
-            tot[a, span(j)] = (
-                snd[a, span(j)].astype(f32) + tot[a, span(j)].astype(f32)
-            ).astype(bf16)
-            total_copy(a, j).start()
-
-    def finish(a, j):
+            for j in range(per_block):
+                end_copy(a, b * per_block + j).start()
+
+    def totals_of(a, b):
         @pl.when(outer)
         def _():
-            total_copy(a, j).wait_recv()
-
-    def service(step):
-        if isinstance(step, int):
-            behind, ahead = divmod(step - LAG, chunks), divmod(step, chunks)
-        else:
-            behind = (lax.div(step - LAG, chunks), lax.rem(step - LAG, chunks))
-            ahead = (lax.div(step, chunks), lax.rem(step, chunks))
-        if not isinstance(step, int) or LAG <= step:
-            relay_b(*behind)
-        if not isinstance(step, int) or step < 4 * chunks:
-            relay_a(*ahead)
-
-    def drain(a):
-        def body(j, carry):
+            for j in range(per_block):
+                total_copy(a, b * per_block + j).wait_recv()
+
+    def drain_all():
+        def body(n, carry):
+            a, j = lax.div(n, chunks), lax.rem(n, chunks)
+
             @pl.when(outer)
             def _():
                 end_copy(a, j).wait_send()
@@ -587,10 +648,21 @@
 
             return carry
 
-        lax.fori_loop(0, chunks, body, 0)
-
-    gather_start(4)
-    gather_start(0)
+        lax.fori_loop(0, 3 * chunks, body, 0)
+
+    for k in range(1, 4):
+        gain_copy(k).start()
+    gain_over(0).start()
+    gather_own(0)
+    gather_own(1)
+    out_copies = [
+        remote(
+            staged.at[3], other_out.at[k - 1], zo_send.at[k - 1], zo_recv.at[k - 1], (f, c, t ^ k)
+        )
+        for k in range(1, 4)
+    ]
+    for copy in out_copies:
+        copy.start()
 
     half = table_ref.shape[1] // 2
     far = half - 1
@@ -625,17 +697,20 @@
                 )
         return carry
 
-    lax.fori_loop(0, keys // BLOCK, bias_rows, 0)
-    near[...] = jnp.zeros_like(near)
-    dk[...] = jnp.zeros_like(dk)
-    dv[...] = jnp.zeros_like(dv)
-    small[...] = jnp.zeros_like(small)
-
-    gather_relay(4)
-    gather_relay(0)
-    for g in (1, 2, 3):
-        gather_start(g)
-    gather_finish(4)
+    key_blocks = keys // BLOCK
+    lax.fori_loop(0, key_blocks // 4, bias_rows, 0)
+    for k in range(1, 4):
+        gain_copy(k).wait_recv()
+        gain_over(k).start()
+    gather_pass(0)
+    lax.fori_loop(key_blocks // 4, key_blocks // 2, bias_rows, 0)
+    gather_pass(1)
+    for copy in loads[4:]:
+        copy.wait()
+    gather_own(2)
+    gather_own(3)
+    for k in range(4):
+        gain_over(k).wait_recv()
     spread = jnp.zeros((8, width), f32)
     for i in range(shards):
         one_hot = (iota((BLOCK, width), 1) == iota((BLOCK, width), 0) + i * shard).astype(f32)
@@ -643,6 +718,8 @@
     gain_rows[...] = spread
 
     def block_rows(b, size=BLOCK):
+        if isinstance(b, int):
+            return pl.ds(b * size, size)
         return pl.ds(pl.multiple_of(b * size, size), size)
 
     def inverse_rms(values):
@@ -655,83 +732,165 @@
         return carry
 
     lax.fori_loop(0, rows // BLOCK, norm_one, 0)
-    gather_finish(0)
 
     def weight(buffer, a):
         return buffer[:, a].reshape(width, buffer.shape[-1])
 
+    own_rows = pl.ds(pl.multiple_of(t * head_width, DH), head_width)
     own_keys = pl.ds(pl.multiple_of(c * rows, rows), rows)
     normed = n1[...]
-    k_all[own_keys, :] = contract(normed, weight(wa, 1), 1, 0).astype(bf16)
-    v_all[own_keys, :] = contract(normed, weight(wa, 2), 1, 0).astype(bf16)
     kv_copies = [
         remote(ref.at[own_keys], ref.at[own_keys], kv_send.at[n], kv_recv.at[n], partner)
         for n, ref in enumerate((k_all, v_all))
     ]
-    for copy in kv_copies:
-        copy.start()
-    q_t[...] = contract(normed, weight(wa, 0), 1, 0).astype(bf16).T
+    gather_corner(0)
+    lax.fori_loop(key_blocks // 2, key_blocks * 3 // 4, bias_rows, 0)
+    gather_finish(0)
+    mixed_kv = contract(normed, wkv[...].reshape(width, 2 * head_width), 1, 0).astype(bf16)
+    k_all[own_keys, :] = mixed_kv[:, 0:head_width]
+    kv_copies[0].start()
+    v_all[own_keys, :] = mixed_kv[:, head_width:]
+    kv_copies[1].start()
+    gather_corner(1)
+    lax.fori_loop(key_blocks * 3 // 4, key_blocks, bias_rows, 0)
     n1t[...] = normed.T
-    gather_relay(1)
+    gather_pass(2)
+    for k in range(1, 4):
+        out_copies[k - 1].wait_recv()
+        wo3[me, :, (k - 1) * head_width : k * head_width] = other_out[k - 1]
+    gather_own(5)
+    gather_own(4)
+    gather_finish(1)
+    q_t[...] = contract(normed, wqo[:, :, 0:head_width].reshape(width, head_width), 1, 0).astype(bf16).T
     for copy in kv_copies:
         copy.wait_recv()
-    k_t[...] = k_all[...].T
     v_t[...] = v_all[...].T
-    gather_finish(1)
-
-    head_of = iota((head_width, QUERY_BLOCK), 0)
 
     def head_only(values, h):
+        head_of = iota(values.shape, 0)
         inside = jnp.logical_and(head_of >= h * DH, head_of < (h + 1) * DH)
         return jnp.where(inside, values, jnp.zeros_like(values))
 
-    def attend(qb, carry):
-        at = block_rows(qb, QUERY_BLOCK)
-        for h in range(heads):
+    def attended_copy(source, b, slot, target):
+        view = att_all.at[
+            pl.ds(pl.multiple_of(source * head_width, DH), head_width), block_rows(b)
+        ]
+        return remote(view, view, at_send.at[slot, b], at_recv.at[source, b], (f, c, target))
+
+    def attended_start(b):
+        @pl.when(outer)
+        def _():
+            attended_copy(t, b, 0, near_end).start()
+
+        @pl.when(inner)
+        def _():
+            attended_copy(t, b, 0, far_end).start()
+            attended_copy(t, b, 1, middle).start()
+
+    def attended_relay(b, part):
+        @pl.when(inner)
+        def _():
+            source = (far_end, middle, 3 - far_end)[part]
+            attended_copy(source, b, 2 + part, middle if part == 0 else far_end).wait_recv()
+            attended_copy(source, b, 2 + part, middle if part == 0 else far_end).start()
+
+    def attended_wait(b):
+        @pl.when(outer)
+        def _():
+            for source in (near_end, 3 - near_end, 3 - t):
+                attended_copy(source, b, 0, near_end).wait_recv()
+
+    def attended_drain(b, carry):
+        attended_copy(t, b, 0, near_end).wait_send()
+
+        @pl.when(inner)
+        def _():
+            for slot in range(1, 5):
+                attended_copy(t, b, slot, middle).wait_send()
+
+        return carry
+
+    def attend(qb):
+        at = block_rows(qb, FORWARD_BLOCK)
+
+        def per_head(h, carry):
             queries = head_only(q_t[:, at], h)
-            top = jnp.full((8, QUERY_BLOCK), -jnp.inf, f32)
+            top = jnp.full((8, FORWARD_BLOCK), -jnp.inf, f32)
             for kb in range(keys // BLOCK):
                 span_k = slice(kb * BLOCK, (kb + 1) * BLOCK)
                 block = contract(k_all[span_k, :], queries, 1, 0) + masked_bias[h, span_k, at]
-                score[span_k, :] = block
-                top = jnp.maximum(top, jnp.max(block.reshape(BLOCK // 8, 8, QUERY_BLOCK), axis=0))
+                score[span_k, 0:FORWARD_BLOCK] = block
+                top = jnp.maximum(top, jnp.max(block.reshape(BLOCK // 8, 8, FORWARD_BLOCK), axis=0))
             top = jnp.max(top, axis=0, keepdims=True)
-            total = jnp.zeros((8, QUERY_BLOCK), f32)
+            total = jnp.zeros((8, FORWARD_BLOCK), f32)
             for kb in range(keys // BLOCK):
                 span_k = slice(kb * BLOCK, (kb + 1) * BLOCK)
-                block = jnp.exp(score[span_k, :] - top)
+                block = jnp.exp(score[span_k, 0:FORWARD_BLOCK] - top)
                 expo[h, span_k, at] = block.astype(bf16)
-                total = total + jnp.sum(block.reshape(BLOCK // 8, 8, QUERY_BLOCK), axis=0)
+                total = total + jnp.sum(block.reshape(BLOCK // 8, 8, FORWARD_BLOCK), axis=0)
             inverse = 1.0 / jnp.sum(total, axis=0, keepdims=True)
-            linv[h : h + 1, at] = inverse
-            mixed = contract(v_t[h * DH : (h + 1) * DH, :], expo[h, :, at], 1, 0)
-            att_t[h * DH : (h + 1) * DH, at] = (mixed * inverse).astype(bf16)
-        attended = att_t[:, at].T
-        snd[0, at, :] = contract(attended, weight(wa, 3), 1, 1).astype(bf16)
-        for j in range(QUERY_BLOCK // CHUNK):
-            put(0, qb * (QUERY_BLOCK // CHUNK) + j)
-        return carry
-
-    lax.fori_loop(0, rows // QUERY_BLOCK, attend, 0)
-
-    for g in (2, 3):
-        gather_relay(g)
-    for g in (2, 3):
-        gather_finish(g)
-
-    per_block = BLOCK // CHUNK
+            linv[h, :, at] = jnp.broadcast_to(inverse, (8, FORWARD_BLOCK))
+            head_rows = pl.ds(pl.multiple_of(h * DH, DH), DH)
+            own_head = pl.ds(pl.multiple_of(t * head_width + h * DH, DH), DH)
+            mixed = contract(v_t[head_rows, :], expo[h, :, at], 1, 0)
+            att_all[own_head, at] = (mixed * inverse).astype(bf16)
+            return carry
+
+        lax.fori_loop(0, heads, per_head, 0)
+        for n in range(FORWARD_BLOCK // BLOCK):
+            attended_start(qb * (FORWARD_BLOCK // BLOCK) + n)
+
     blocks = rows // BLOCK
     scale = 0.7978845608028654
-    for step in range(LAG):
-        service(step)
+    forward_blocks = rows // FORWARD_BLOCK
+
+    def attend_loop(qb, carry):
+        attend(qb)
+
+        @pl.when(qb == 0)
+        def _():
+            gather_pass(3)
+
+        return carry
+
+    lax.fori_loop(0, forward_blocks, attend_loop, 0)
+    per_forward = FORWARD_BLOCK // BLOCK
+    for b in range(per_forward):
+        attended_relay(b, 0)
+        attended_relay(b, 1)
+    gather_corner(2)
+    gather_pass(5)
+    gather_pass(4)
+    for b in range(per_forward):
+        attended_relay(b, 2)
+    gather_corner(3)
+    wo_all[t] = wqo[:, :, head_width:].reshape(width, head_width)
+    for first in range(per_forward, blocks, per_forward):
+        for b in range(first, first + per_forward):
+            attended_relay(b, 0)
+            attended_relay(b, 1)
+        for b in range(first, first + per_forward):
+            attended_relay(b, 2)
+    near[...] = jnp.zeros_like(near)
+    dk[...] = jnp.zeros_like(dk)
+    dv[...] = jnp.zeros_like(dv)
+    small[...] = jnp.zeros_like(small)
+    k_t[...] = k_all[...].T
+    gather_corner(5)
+    gather_corner(4)
+    gather_finish(5)
+    for k in range(1, 4):
+        wo_all[t ^ k] = wo3[:, :, (k - 1) * head_width : k * head_width].reshape(width, head_width)
+    for g in (2, 3, 4):
+        gather_finish(g)
 
     def feed_forward(b, carry):
-        for j in range(per_block):
-            service(b * per_block + LAG + j)
-        for j in range(per_block):
-            finish(0, b * per_block + j)
+        attended_wait(b)
         at = block_rows(b)
-        res = x_ref[at, :].astype(f32) + tot[0, at, :].astype(f32)
+        res = x_ref[at, :].astype(f32)
+        for source in range(4):
+            attended = att_all[source * head_width : (source + 1) * head_width, at].T
+            res = res + contract(attended, wo_all[source], 1, 1)
         resid[at, :] = res
         normed = (res * inverse_rms(res) * gain_rows[1:2, :]).astype(bf16)
         n2[at, :] = normed
@@ -750,24 +909,27 @@
         act[at, :] = low_act
         ggate[at, :] = low_gate
         gup[at, :] = low_up
-        snd[1, at, :] = (
+        snd[0, at, :] = (
             contract(low_gate, weight(wf, 0), 1, 1) + contract(low_up, weight(wf, 1), 1, 1)
         ).astype(bf16)
-        for j in range(per_block):
-            put(1, b * per_block + j)
-        snd[2, at, :] = contract(low_act, down, 1, 1).astype(bf16)
+        put_block(0, b)
+        snd[1, at, :] = contract(low_act, down, 1, 1).astype(bf16)
+
+        @pl.when(b > 0)
+        def _():
+            serve((b - 1) * per_block, per_block)
+
         return carry
 
-    lax.fori_loop(0, rows // BLOCK, feed_forward, 0)
-
-    def put_all(a):
-        def body(j, carry):
-            put(a, j)
-            return carry
-
-        lax.fori_loop(0, chunks, body, 0)
-
-    put_all(2)
+    lax.fori_loop(0, blocks, feed_forward, 0)
+
+    def put_outputs(b, carry):
+        put_block(1, b)
+        return carry
+
+    lax.fori_loop(0, blocks, put_outputs, 0)
+    turned[0] = n2[...].T
+    turned[1] = cot_ref[...].T
 
     def sent(n, which):
         if n == 0:
@@ -793,11 +955,15 @@
         )
 
     members_of = {0: (0, 1, 2), 1: (3,), 2: (0, 1, 2)}
-    results = {
-        0: (gg_ref, gu_ref, gd_ref),
-        1: (go_ref,),
-        2: (gq_ref, gk_ref, gv_ref),
-    }
+    outputs = {0: (gg_hbm, gu_hbm, gd_hbm), 1: (go_hbm,), 2: (gk_hbm, gv_hbm, gq_hbm)}
+
+    def part_stores(n):
+        results = gf_ref if n == 0 else ga_ref
+        offset = (0, 3, 4)[n]
+        return [
+            pltpu.make_async_copy(results.at[a], target, store_sem.at[offset + i])
+            for i, (a, target) in enumerate(zip(members_of[n], outputs[n]))
+        ]
 
     def reduce_send(n):
         over_copy(n).wait_recv()
@@ -819,11 +985,14 @@
         total, got = (sf, rf2) if n == 0 else (sa, ra2)
         for k in range(1, groups):
             out_copy(n, k).wait_recv()
-        for a, result in zip(members_of[n], results[n]):
+        results = gf_ref if n == 0 else ga_ref
+        for a in members_of[n]:
             value = total[f, a].astype(f32)
             for k in range(1, groups):
                 value = value + got[k - 1, a].astype(f32)
-            result[...] = value
+            results[a] = value
+        for copy in part_stores(n):
+            copy.start()
 
     def reduce_drain(n):
         over_copy(n).wait_send()
@@ -835,18 +1004,19 @@
     def store_grad(buffer, i, a, value):
         buffer[i, :, a] = value.astype(bf16).reshape(2, shard, value.shape[-1])
 
+    def pair_rows(i):
+        return block_rows(i, both)
+
     def feed_forward_weights(i):
-        cut = slice(i * both, (i + 1) * both)
-        n2_t = n2[:, cut].T
-        store_grad(gsf, i, 0, contract(n2_t, ggate[...], 1, 0))
-        store_grad(gsf, i, 1, contract(n2_t, gup[...], 1, 0))
-        store_grad(gsf, i, 2, contract(cot_ref[:, cut].T, act[...], 1, 0))
+        at = pair_rows(i)
+        store_grad(gsf, i, 0, contract(turned[0, at, :], ggate[...], 1, 0))
+        store_grad(gsf, i, 1, contract(turned[0, at, :], gup[...], 1, 0))
+        store_grad(gsf, i, 2, contract(turned[1, at, :], act[...], 1, 0))
 
     def residual_back(b):
-        for j in range(per_block):
-            finish(1, b * per_block + j)
+        totals_of(0, b)
         at = block_rows(b)
-        grad_in = tot[1, at, :].astype(f32)
+        grad_in = tot[0, at, :].astype(f32)
         res = resid[at, :]
         inverse = inverse_rms(res)
         u = res * inverse
@@ -858,48 +1028,52 @@
         grad_res[at, :] = grad
         low_grad = grad.astype(bf16)
         grl[at, :] = low_grad
-        grad_att = contract(low_grad, weight(wa, 3), 1, 0).astype(bf16)
+        grad_att = contract(low_grad, wo_all[t], 1, 0).astype(bf16)
         scaled = grad_att.T.astype(f32) * jnp.concatenate(
-            [jnp.broadcast_to(linv[h : h + 1, at], (DH, BLOCK)) for h in range(heads)], axis=0
+            [jnp.broadcast_to(linv[h, 0:1, at], (DH, BLOCK)) for h in range(heads)], axis=0
         )
         scaled = scaled.astype(bf16)
         dos_t[:, at] = scaled
-        delta[0:heads, at] = jnp.sum(
-            (scaled.astype(f32) * att_t[:, at].astype(f32)).reshape(heads, DH, BLOCK), axis=1
-        )
+        products = scaled.astype(f32) * att_all[own_rows, at].astype(f32)
+        for h in range(heads):
+            delta[h, :, at] = jnp.broadcast_to(
+                jnp.sum(products[h * DH : (h + 1) * DH], axis=0, keepdims=True), (8, BLOCK)
+            )
 
     extra = dk.shape[1] - head_width
     query_blocks = rows // BLOCK
 
-    def attend_back(qb, h):
-        at = block_rows(qb, QUERY_BLOCK)
+    def attend_back(start, size, h):
+        at = slice(start, start + size)
+        first = start // BLOCK
+        head_rows = pl.ds(pl.multiple_of(h * DH, DH), DH)
         if True:
             grads = head_only(dos_t[:, at], h)
             queries = head_only(q_t[:, at], h)
-            flag = iota((extra, QUERY_BLOCK), 0)
-            lane = iota((extra, QUERY_BLOCK), 1)
-            flags = jnp.zeros((extra, QUERY_BLOCK), f32)
-            for j in range(QUERY_BLOCK // BLOCK):
+            flag = iota((extra, size), 0)
+            lane = iota((extra, size), 1)
+            flags = jnp.zeros((extra, size), f32)
+            for j in range(size // BLOCK):
                 hit = jnp.logical_and(
-                    flag == h * query_blocks + qb * (QUERY_BLOCK // BLOCK) + j,
+                    flag == h * query_blocks + first + j,
                     jnp.logical_and(lane >= j * BLOCK, lane < (j + 1) * BLOCK),
                 )
                 flags = jnp.where(hit, 1.0, flags)
             flagged = jnp.concatenate([queries, flags.astype(bf16)], axis=0)
-            shift = delta[h : h + 1, at]
+            shift = delta[h, 0:1, at]
             for kb in range(keys // BLOCK):
                 span_k = slice(kb * BLOCK, (kb + 1) * BLOCK)
                 block = contract(v_all[span_k, :], grads, 1, 0)
-                low_score[span_k, :] = (
+                low_score[span_k, 0:size] = (
                     expo[h, span_k, at].astype(f32) * (block - shift)
                 ).astype(bf16)
             dv[...] += contract(expo[h, :, at], grads, 1, 1)
-            dk[...] += contract(low_score[...], flagged, 1, 1)
-            dq_t[h * DH : (h + 1) * DH, at] = contract(
-                k_t[h * DH : (h + 1) * DH, :], low_score[...], 1, 0
+            dk[...] += contract(low_score[:, 0:size], flagged, 1, 1)
+            dq_t[head_rows, at] = contract(
+                k_t[head_rows, :], low_score[:, 0:size], 1, 0
             ).astype(bf16)
-            for j in range(QUERY_BLOCK // BLOCK):
-                home = c * query_blocks + qb * (QUERY_BLOCK // BLOCK) + j
+            for j in range(size // BLOCK):
+                home = c * query_blocks + first + j
                 for d in (-1, 0, 1):
                     kb = home + d
                     valid = jnp.logical_and(kb >= 0, kb < keys // BLOCK)
@@ -911,28 +1085,27 @@
                             block_rows(where_k), j * BLOCK : (j + 1) * BLOCK
                         ].astype(f32)
 
-    served = [blocks * per_block + LAG]
-
-    def serve_to(end):
-        while served[0] < end:
-            service(served[0])
-            served[0] += 1
-
-    weight_parts = list(range(groups))
-    ratio = QUERY_BLOCK // BLOCK
+    pace = per_block // 2
+    step = (blocks - 1) * per_block
     for qb in range(rows // QUERY_BLOCK):
-        for b in range(qb * ratio, (qb + 1) * ratio):
-            serve_to(chunks + (b + 1) * per_block + LAG)
+        for b in range(qb * QUERY_BLOCK // BLOCK, (qb + 1) * QUERY_BLOCK // BLOCK):
+            need = max((b + 1) * per_block + LAG, step)
+            serve(step, need - step)
+            step = need
             residual_back(b)
-        for h in range(heads):
-            attend_back(qb, h)
-            if weight_parts:
-                feed_forward_weights(weight_parts.pop(0))
-            if qb + 1 < rows // QUERY_BLOCK or h + 1 < heads:
-                serve_to(served[0] + 1)
+
+        def back_head(h, carry, qb=qb, step=step):
+            attend_back(qb * QUERY_BLOCK, QUERY_BLOCK, h)
+            if qb == 0:
+                feed_forward_weights(h)
+            serve(h * pace + step, pace)
+            return carry
+
+        lax.fori_loop(0, heads, back_head, 0)
+        step += heads * pace
         if qb == 0:
-            while weight_parts:
-                feed_forward_weights(weight_parts.pop(0))
+            for i in range(heads, groups):
+                feed_forward_weights(i)
             over_copy(0).start()
 
     other_keys = pl.ds(pl.multiple_of((1 - c) * rows, rows), rows)
@@ -942,46 +1115,51 @@
     dkv_copy.start()
     reduce_send(0)
     dkv_copy.wait_recv()
-    dkv[0] = (dk[own_keys, 0:head_width] + dkv_recv[0].astype(f32)).astype(bf16)
-    dkv[1] = (dv[own_keys, :] + dkv_recv[1].astype(f32)).astype(bf16)
-
-    def project_back(b):
+    dkv[:, 0:head_width] = (dk[own_keys, 0:head_width] + dkv_recv[0].astype(f32)).astype(bf16)
+    dkv[:, head_width:] = (dv[own_keys, :] + dkv_recv[1].astype(f32)).astype(bf16)
+
+    def project_back(b, carry):
         at = block_rows(b)
-        total = contract(dq_t[:, at].T, weight(wa, 0), 1, 1)
-        total = total + contract(dkv[0, at, :], weight(wa, 1), 1, 1)
-        total = total + contract(dkv[1, at, :], weight(wa, 2), 1, 1)
-        snd[3, at, :] = total.astype(bf16)
-        for j in range(per_block):
-            put(3, b * per_block + j)
-
-    for b in range(blocks):
-        project_back(b)
-        serve_to(served[0] + 1)
-
-    grl_t = grl[...].T
-    for i in range(groups):
-        cut = slice(i * both, (i + 1) * both)
-        store_grad(gsa, i, 3, contract(grl_t[cut], att_t[...], 1, 1))
+        total = contract(
+            dq_t[:, at].T, wqo[:, :, 0:head_width].reshape(width, head_width), 1, 1
+        )
+        total = total + contract(dkv[at, :], wkv[...].reshape(width, 2 * head_width), 1, 1)
+        snd[2, at, :] = total.astype(bf16)
+        put_block(2, b)
+
+        @pl.when(step + (b + 1) * pace <= 2 * chunks)
+        def _():
+            serve(step + b * pace, pace)
+
+        return carry
+
+    lax.fori_loop(0, blocks, project_back, 0)
+    step += min(blocks, (2 * chunks - step) // pace) * pace
+
+    def weights_back(i, carry):
+        part_rows = n1t[pair_rows(i), :]
+        mixed = contract(part_rows, dkv[...], 1, 0)
+        store_grad(gsa, i, 0, mixed[:, 0:head_width])
+        store_grad(gsa, i, 1, mixed[:, head_width:])
+        store_grad(gsa, i, 2, contract(part_rows, dq_t[...], 1, 1))
+        return carry
+
+    lax.fori_loop(0, groups, weights_back, 0)
+    over_copy(2).start()
+    serve(step, 2 * chunks - step)
+    step = 2 * chunks
+    turned[0] = grl[...].T
+
+    def output_weights(i, carry):
+        store_grad(gsa, i, 3, contract(turned[0, pair_rows(i), :], att_all[own_rows, :], 1, 1))
+        return carry
+
+    lax.fori_loop(0, groups, output_weights, 0)
     over_copy(1).start()
-    serve_to(3 * chunks + 1)
-
-    def weights_back(i):
-        cut = n1t[i * both : (i + 1) * both, :]
-        store_grad(gsa, i, 0, contract(cut, dq_t[...], 1, 1))
-        store_grad(gsa, i, 1, contract(cut, dkv[0], 1, 0))
-        store_grad(gsa, i, 2, contract(cut, dkv[1], 1, 0))
-
-    for i in range(groups):
-        weights_back(i)
-        if i % 2:
-            serve_to(served[0] + 1)
-    over_copy(2).start()
+    reduce_send(2)
     reduce_send(1)
-    serve_to(served[0] + 1)
-    reduce_send(2)
-    serve_to(served[0] + 1)
-
-    def bucket_sums(h):
+
+    def bucket_sums(h, carry):
         for b in range(2 * half):
             summed_block = jnp.zeros((8, BLOCK), f32)
             for d in (-1, 0) if b < half else (0, 1):
@@ -993,6 +1171,7 @@
             pick[b : b + 1, :] = jnp.sum(summed_block, axis=0, keepdims=True)
         sums = contract(jnp.ones((8, BLOCK), f32), pick[...], 1, 1, highest)
         small[:, 0 : 2 * half] += jnp.where(iota((8, 2 * half), 0) == 2 + h, sums, 0.0)
+        return carry
 
     def far_sums():
         tail = dk.shape[1] - BLOCK
@@ -1022,38 +1201,28 @@
                 + contract(jnp.broadcast_to(right_sum, (8, BLOCK)), right_pick, 1, 0, highest)
             )[0:1]
 
+    def block_store(n, source, target, b):
+        at = block_rows(b)
+        return pltpu.make_async_copy(source.at[at], target.at[at], store_sem.at[n])
+
     def input_back(b):
-        for j in range(per_block):
-            finish(3, b * per_block + j)
+        totals_of(2, b)
         at = block_rows(b)
-        grad_in = tot[3, at, :].astype(f32)
+        grad_in = tot[2, at, :].astype(f32)
         xs = x_ref[at, :].astype(f32)
         inverse = inverse_rms(xs)
         u = xs * inverse
-        small[0:1, :] += jnp.sum(grad_in * u, axis=0, keepdims=True)
         g = grad_in * gain_rows[0:1, :]
         gin_ref[at, :] = grad_res[at, :] + inverse * (
             g - u * jnp.mean(g * u, axis=-1, keepdims=True)
         )
+        block_store(7 + b, gin_ref, gin_hbm, b).start()
 
     def layer_out(b):
-        for j in range(per_block):
-            finish(2, b * per_block + j)
+        totals_of(1, b)
         at = block_rows(b)
-        out_ref[at, :] = (resid[at, :] + tot[2, at, :].astype(f32)).astype(bf16)
-
-    fillers = [functools.partial(bucket_sums, h) for h in range(heads)] + [far_sums]
-    fillers += [functools.partial(layer_out, b) for b in range(blocks)]
-    fillers += [functools.partial(reduce_finish, n) for n in range(2)]
-    for b in range(blocks):
-        need = 3 * chunks + (b + 1) * per_block + LAG
-        while served[0] < need:
-            serve_to(served[0] + 1)
-            if fillers and served[0] < need:
-                fillers.pop(0)()
-        input_back(b)
-        if fillers and b + 1 < blocks:
-            fillers.pop(0)()
+        out_ref[at, :] = (resid[at, :] + tot[1, at, :].astype(f32)).astype(bf16)
+        block_store(7 + blocks + b, out_ref, out_hbm, b).start()
 
     small_copies = [
         remote(
@@ -1064,33 +1233,97 @@
         for kc in range(2)
         if k or kc
     ]
-    for copy in small_copies:
-        copy.start()
-
-    while fillers:
-        fillers.pop(0)()
-    reduce_finish(2)
-    small_all[me] = small[...]
-    for copy in small_copies:
-        copy.wait_recv()
-    total_small = small_all[0]
-    for i in range(1, shards):
-        total_small = total_small + small_all[i]
-    to_own = (iota((width, BLOCK), 0) == iota((width, BLOCK), 1) + me * shard).astype(f32)
-    own_gains = contract(total_small, to_own, 1, 0, highest)
-    gain_one_out_ref[...] = own_gains[0:1, 0:shard]
-    gain_two_out_ref[...] = own_gains[1:2, 0:shard]
-    bias_out_ref[...] = total_small[2 : 2 + heads, 0 : 2 * half]
-
-    for copy in small_copies:
+
+    def small_start():
+        for copy in small_copies:
+            copy.start()
+        small_all[me] = small[...]
+
+    def small_finish():
+        for copy in small_copies:
+            copy.wait_recv()
+        total_small = small_all[0]
+        for i in range(1, shards):
+            total_small = total_small + small_all[i]
+        to_own = (iota((width, BLOCK), 0) == iota((width, BLOCK), 1) + me * shard).astype(f32)
+        own_gains = contract(total_small, to_own, 1, 0, highest)
+        gain_two_out_ref[...] = own_gains[1:2, 0:shard]
+        bias_out_ref[...] = total_small[2 : 2 + heads, 0 : 2 * half]
+
+    gain_copies = [
+        remote(
+            gain_part.at[t], gain_part.at[t], gp_send.at[kt - 1], gp_recv.at[kt - 1], (f, c, t ^ kt)
+        )
+        for kt in range(1, 4)
+    ]
+
+    def gain_start():
+        products = jnp.zeros((shard, head_width), f32)
+        for a in members_of[2]:
+            products = products + staged[a].astype(f32) * ga_ref[a]
+        row_sums = contract(jnp.ones((8, head_width), f32), products, 1, 1, highest)
+        gain_part[t, :, 0:shard] = row_sums / gain_one_ref[...].astype(f32)
+        for copy in gain_copies:
+            copy.start()
+
+    def gain_finish():
+        for copy in gain_copies:
+            copy.wait_recv()
+        total = gain_part[0, 0:1, 0:shard]
+        for i in range(1, 4):
+            total = total + gain_part[i, 0:1, 0:shard]
+        gain_one_out_ref[...] = total
+
+    lax.fori_loop(0, heads, bucket_sums, 0)
+    far_sums()
+    small_start()
+    reduce_finish(0)
+    serve(step, LAG)
+
+    def last_rows(b, carry):
+        serve(2 * chunks + b * per_block + LAG, per_block)
+
+        @pl.when(b == LATE_BLOCK)
+        def _():
+            small_finish()
+            reduce_finish(1)
+
+        @pl.when(b == LATE_BLOCK + 1)
+        def _():
+            reduce_finish(2)
+            gain_start()
+
+        @pl.when(b == blocks - 1)
+        def _():
+            gain_finish()
+
+        layer_out(b)
+        input_back(b)
+        return carry
+
+    lax.fori_loop(0, blocks, last_rows, 0)
+
+    for b in range(blocks):
+        block_store(7 + b, gin_ref, gin_hbm, b).wait()
+        block_store(7 + blocks + b, out_ref, out_hbm, b).wait()
+    for n in range(3):
+        for copy in part_stores(n):
+            copy.wait()
+    for copy in small_copies + gain_copies:
         copy.wait_send()
-    for g in range(5):
+    for g in range(6):
         gather_drain(g)
+    for copy in out_copies:
+        copy.wait_send()
+    lax.fori_loop(0, blocks, attended_drain, 0)
+    for k in range(1, 4):
+        gain_copy(k).wait_send()
+    for k in range(4):
+        gain_over(k).wait_send()
     for copy in kv_copies:
         copy.wait_send()
     dkv_copy.wait_send()
-    for a in range(4):
-        drain(a)
+    drain_all()
     for n in range(3):
         reduce_drain(n)
 
@@ -1117,8 +1350,20 @@
         jax.ShapeDtypeStruct(table.shape, f32),
     )
     in_vmem = pl.BlockSpec(memory_space=pltpu.VMEM)
+    anywhere = pl.BlockSpec(memory_space=pl.ANY)
     scratch = [
-        vmem((shards, 4, shard, head_width), bf16),
+        vmem((rows, width), bf16),
+        vmem((rows, width), bf16),
+        vmem((rows, width), bf16),
+        vmem((rows, width), f32),
+        vmem((4, shard, head_width), f32),
+        vmem((3, shard, units), f32),
+        vmem((4, shard, head_width), bf16),
+        vmem((shards, shard, 2 * head_width), bf16),
+        vmem((shards, shard, 2 * head_width), bf16),
+        vmem((shards, shard, 3 * head_width), bf16),
+        vmem((3, shard, head_width), bf16),
+        vmem((4, width, head_width), bf16),
         vmem((shards, 3, shard, units), bf16),
         vmem((shards, 8, BLOCK), f32),
         vmem((8, width), f32),
@@ -1127,15 +1372,16 @@
         vmem((keys, QUERY_BLOCK), f32),
         vmem((heads, keys, rows), bf16),
         vmem((keys, QUERY_BLOCK), bf16),
-        vmem((4, rows, width), bf16),
-        vmem((4, rows, width), bf16),
-        vmem((4, rows, width), bf16),
+        vmem((3, rows, width), bf16),
+        vmem((3, rows, width), bf16),
+        vmem((3, rows, width), bf16),
         vmem((rows, width), f32),
         vmem((rows, width), f32),
         vmem((rows, width), bf16),
         vmem((rows, width), bf16),
         vmem((rows, width), bf16),
         vmem((width, rows), bf16),
+        vmem((2, width, rows), bf16),
         vmem((rows, units), bf16),
         vmem((rows, units), bf16),
         vmem((rows, units), bf16),
@@ -1144,18 +1390,18 @@
         vmem((keys, head_width), bf16),
         vmem((head_width, keys), bf16),
         vmem((head_width, keys), bf16),
+        vmem((4 * head_width, rows), bf16),
         vmem((head_width, rows), bf16),
         vmem((head_width, rows), bf16),
-        vmem((head_width, rows), bf16),
-        vmem((8, rows), f32),
-        vmem((8, rows), f32),
+        vmem((heads, 8, rows), f32),
+        vmem((heads, 8, rows), f32),
         vmem((keys, padded), f32),
         vmem((keys, head_width), f32),
         vmem((heads, 3, BLOCK, BLOCK), f32),
         vmem((table.shape[1], BLOCK), f32),
         vmem((2, rows, head_width), bf16),
         vmem((2, rows, head_width), bf16),
-        vmem((2, rows, head_width), bf16),
+        vmem((rows, 2 * head_width), bf16),
         vmem((groups, 2, 4, shard, head_width), bf16),
         vmem((groups, 2, 3, shard, units), bf16),
         vmem((groups, 4, shard, head_width), bf16),
@@ -1166,14 +1412,21 @@
         vmem((groups - 1, 3, shard, units), bf16),
         vmem((8, width), f32),
         vmem((shards, 8, width), f32),
-        dma((5, 2 * groups)),
-        dma((5, 2 * groups)),
+        vmem((4, 8, BLOCK), f32),
+        dma((9,)),
+        dma((7 + 2 * (rows // BLOCK),)),
+        dma((7, 8)),
+        dma((7, 8)),
+        dma((3,)),
+        dma((3,)),
+        dma((5, rows // BLOCK)),
+        dma((4, rows // BLOCK)),
         dma((2,)),
         dma((2,)),
-        dma((4, chunks)),
-        dma((4, chunks)),
-        dma((4, chunks)),
-        dma((4, chunks)),
+        dma((3, chunks)),
+        dma((3, chunks)),
+        dma((3, chunks)),
+        dma((3, chunks)),
         dma((1,)),
         dma((1,)),
         dma((3,)),
@@ -1182,12 +1435,17 @@
         dma((3, groups)),
         dma((shards,)),
         dma((shards,)),
+        dma((3,)),
+        dma((3,)),
     ]
     return pl.pallas_call(
         functools.partial(layer_kernel, shards),
         out_shape=out_shape,
-        in_specs=[in_vmem] * 12 + [pl.BlockSpec(memory_space=pltpu.SMEM)],
-        out_specs=[in_vmem] * len(out_shape),
+        in_specs=[anywhere] * 2
+        + [in_vmem] * 3
+        + [anywhere] * 7
+        + [pl.BlockSpec(memory_space=pltpu.SMEM)],
+        out_specs=[anywhere] * 9 + [in_vmem] * 3,
         scratch_shapes=scratch,
         name="layer",
         compiler_params=pltpu.CompilerParams(
@@ -1274,7 +1532,7 @@
 
 
 def fits_kernel(mesh):
-    return mesh.shape["ctx"] == 2 and mesh.shape["tp"] == 4 and mesh.shape["fsdp"] in (2, 4)
+    return mesh.shape["ctx"] == 2 and mesh.shape["tp"] == 4 and mesh.shape["fsdp"] == 4
 
 
 def solution(mesh):

time: 122 us -> 112 us (0.918)
  Pallas kernels: 121 us -> 111 us
    pallas_call x1, Pallas kernels: 117 us -> 107 us  [fused_layer(): pl.pallas_call(functools.partial(layer_kernel, shards), out_shape=out_sha...]
where the time goes in v3:
time: 112 us; the launch traced here: 111 us
  Pallas kernels  111 us (99%)
    pallas_call x1, Pallas kernels, fused_layer(): pl.pallas_call(functools.partial(layer_kernel, shards), out_shape=out_sha...  107 us
    pallas_call x1, Pallas kernels, publish(): pl.pallas_call(functools.partial(publish_kernel, count), out_shape=[jax.S...  3.33 us

profile of v3, /device:TPU:0, one launch (start us, length us, event | category | flops | bytes accessed | tf_op | source)
XLA Modules:
  0.0 111.4 jit_solution(6382838872691315555)
XLA Ops:
  0.6 107.2 %layer.1 = (bf16[512,768]{1,0:T(8,128)(2,1)}, f32[512,768]{1,0:T(8,128)}, f32[96,192]{1,0:T(8,128)}, f32[96,192]{1,0:T(8,128)}, f32[96,192]{1,0:T(8,128)}, /*ind...) custom-call(bf16[512,768]{1,0:T(8,128)(2,1)} %bitcast.10, ...), custom_call_target="tpu_custom_call" | custom-call | tf_op jit(solution)/shard_map/layer/pallas_call | solution.py:1441
  107.9 3.3 %publish.1 = (bf16[512,768]{1,0:T(8,128)(2,1)}, f32[512,768]{1,0:T(8,128)}, f32[96,192]{1,0:T(8,128)}, f32[96,192]{1,0:T(8,128)}, f32[96,192]{1,0:T(8,128)}, /*i...) custom-call(bf16[512,768]{1,0:T(8,128)(2,1)} %get-tuple-element.36.r, ...), custom_call_target="tpu_custom_call" | custom-call | tf_op jit(solution)/shard_map/publish/pallas_call | solution.py:1478

commit v4 on v3

--- a/solution.py
+++ b/solution.py
@@ -307,8 +307,9 @@
 FORWARD_BLOCK = 256
 CHUNK = 32
 LAG = 4
-RELAY_ROWS = 16
-LATE_BLOCK = 1
+RELAY_ROWS = 32
+EARLY = 4
+PACES = (1, 1, 1)
 
 
 def contract(left, right, left_dim, right_dim, precision=None):
@@ -590,6 +591,15 @@
 
         lax.fori_loop(0, CHUNK // RELAY_ROWS, body, 0)
 
+    def flush(first, last):
+        @pl.when(inner)
+        def _():
+            for n in range(first, last):
+                a, j = divmod(n, chunks)
+                mid_copy(a, j).wait_recv()
+                add_rows(tot, a, j, snd, tot)
+                total_copy(a, j).start()
+
     def service(step):
         def total_step():
             a, j = split(step - LAG)
@@ -609,12 +619,14 @@
             return lax.div(n, chunks), lax.rem(n, chunks)
 
         if isinstance(step, int):
-            if step >= LAG:
+            if step >= LAG and not chunks <= step < chunks + LAG:
                 pl.when(inner)(total_step)
             if step < 3 * chunks:
                 pl.when(inner)(middle_step)
         else:
-            pl.when(jnp.logical_and(inner, step >= LAG))(total_step)
+            flushed = jnp.logical_and(step >= chunks, step < chunks + LAG)
+            due = jnp.logical_and(step >= LAG, jnp.logical_not(flushed))
+            pl.when(jnp.logical_and(inner, due))(total_step)
             pl.when(jnp.logical_and(inner, step < 3 * chunks))(middle_step)
 
     def serve(start, count):
@@ -855,32 +867,34 @@
 
     lax.fori_loop(0, forward_blocks, attend_loop, 0)
     per_forward = FORWARD_BLOCK // BLOCK
-    for b in range(per_forward):
-        attended_relay(b, 0)
-        attended_relay(b, 1)
+    early = range(per_forward)
+    late = range(per_forward, blocks)
+
+    def relays(group, part):
+        for b in group:
+            attended_relay(b, part)
+
     gather_corner(2)
+    near[...] = jnp.zeros_like(near)
+    wo_all[t] = wqo[:, :, head_width:].reshape(width, head_width)
     gather_pass(5)
+    relays(early, 0)
+    relays(early, 1)
     gather_pass(4)
-    for b in range(per_forward):
-        attended_relay(b, 2)
     gather_corner(3)
-    wo_all[t] = wqo[:, :, head_width:].reshape(width, head_width)
-    for first in range(per_forward, blocks, per_forward):
-        for b in range(first, first + per_forward):
-            attended_relay(b, 0)
-            attended_relay(b, 1)
-        for b in range(first, first + per_forward):
-            attended_relay(b, 2)
-    near[...] = jnp.zeros_like(near)
+    relays(late, 0)
+    relays(late, 1)
+    gather_corner(5)
+    relays(early, 2)
+    gather_corner(4)
+    k_t[...] = k_all[...].T
     dk[...] = jnp.zeros_like(dk)
     dv[...] = jnp.zeros_like(dv)
     small[...] = jnp.zeros_like(small)
-    k_t[...] = k_all[...].T
-    gather_corner(5)
-    gather_corner(4)
     gather_finish(5)
     for k in range(1, 4):
         wo_all[t ^ k] = wo3[:, :, (k - 1) * head_width : k * head_width].reshape(width, head_width)
+    relays(late, 2)
     for g in (2, 3, 4):
         gather_finish(g)
 
@@ -1087,33 +1101,46 @@
 
     pace = per_block // 2
     step = (blocks - 1) * per_block
-    for qb in range(rows // QUERY_BLOCK):
-        for b in range(qb * QUERY_BLOCK // BLOCK, (qb + 1) * QUERY_BLOCK // BLOCK):
-            need = max((b + 1) * per_block + LAG, step)
-            serve(step, need - step)
-            step = need
+
+    query_parts = [(start, QUERY_BLOCK) for start in range(0, rows - QUERY_BLOCK, QUERY_BLOCK)]
+    query_parts += [(start, BLOCK) for start in range(rows - QUERY_BLOCK, rows, BLOCK)]
+    for qb, (start, size) in enumerate(query_parts):
+        for b in range(start // BLOCK, (start + size) // BLOCK):
             residual_back(b)
-
-        def back_head(h, carry, qb=qb, step=step):
-            attend_back(qb * QUERY_BLOCK, QUERY_BLOCK, h)
             if qb == 0:
-                feed_forward_weights(h)
-            serve(h * pace + step, pace)
+                service(step)
+                step += 1
+
+        def back_head(h, carry, start=start, size=size, step=step, qb=qb):
+            attend_back(start, size, h)
+            serve(h * PACES[qb] + step, PACES[qb])
             return carry
 
         lax.fori_loop(0, heads, back_head, 0)
-        step += heads * pace
+        step += heads * PACES[qb]
         if qb == 0:
-            for i in range(heads, groups):
+
+            def early_weights(i, carry, step=step):
                 feed_forward_weights(i)
+
+                @pl.when(i < EARLY)
+                def _():
+                    service(i + step)
+
+                return carry
+
+            lax.fori_loop(0, groups, early_weights, 0)
+            step += EARLY
             over_copy(0).start()
+            flush(chunks - LAG, chunks)
+        if qb == 1:
+            reduce_send(0)
 
     other_keys = pl.ds(pl.multiple_of((1 - c) * rows, rows), rows)
     dkv_send[0] = dk[other_keys, 0:head_width].astype(bf16)
     dkv_send[1] = dv[other_keys, :].astype(bf16)
     dkv_copy = remote(dkv_send.at[...], dkv_recv.at[...], dkv_ssem.at[0], dkv_rsem.at[0], partner)
     dkv_copy.start()
-    reduce_send(0)
     dkv_copy.wait_recv()
     dkv[:, 0:head_width] = (dk[own_keys, 0:head_width] + dkv_recv[0].astype(f32)).astype(bf16)
     dkv[:, head_width:] = (dv[own_keys, :] + dkv_recv[1].astype(f32)).astype(bf16)
@@ -1274,35 +1301,47 @@
             total = total + gain_part[i, 0:1, 0:shard]
         gain_one_out_ref[...] = total
 
-    lax.fori_loop(0, heads, bucket_sums, 0)
-    far_sums()
-    small_start()
-    reduce_finish(0)
-    serve(step, LAG)
-
-    def last_rows(b, carry):
-        serve(2 * chunks + b * per_block + LAG, per_block)
-
-        @pl.when(b == LATE_BLOCK)
+    @pl.when(outer)
+    def _():
+        lax.fori_loop(0, heads, bucket_sums, 0)
+        far_sums()
+
+    def at_step(n, value, run):
+        pl.when(n == value)(run)
+
+    def last_steps(n, carry):
+        service(2 * chunks + n)
+
+        @pl.when(jnp.logical_and(inner, jnp.logical_and(lax.rem(n, 2) == 0, n < 2 * heads)))
         def _():
-            small_finish()
-            reduce_finish(1)
-
-        @pl.when(b == LATE_BLOCK + 1)
+            bucket_sums(lax.div(n, 2), 0)
+
+        pl.when(jnp.logical_and(inner, n == 2 * heads))(far_sums)
+        at_step(n, 2 * heads + 1, small_start)
+        at_step(n, 2 * heads + 2, functools.partial(reduce_finish, 0))
+
+        @pl.when(jnp.logical_and(n > 2 * heads + 2, n <= 2 * heads + 2 + blocks))
         def _():
+            layer_out(n - 2 * heads - 3)
+
+        def gains():
             reduce_finish(2)
             gain_start()
 
-        @pl.when(b == blocks - 1)
+        at_step(n, 2 * heads + 3 + blocks, gains)
+        at_step(n, 2 * heads + 4 + blocks, small_finish)
+        at_step(n, 2 * heads + 5 + blocks, functools.partial(reduce_finish, 1))
+        at_step(n, chunks + LAG - 2, gain_finish)
+
+        due = n - (per_block - 1) - LAG
+
+        @pl.when(jnp.logical_and(due >= 0, lax.rem(due, per_block) == 0))
         def _():
-            gain_finish()
-
-        layer_out(b)
-        input_back(b)
+            input_back(lax.div(due, per_block))
+
         return carry
 
-    lax.fori_loop(0, blocks, last_rows, 0)
-
+    lax.fori_loop(0, chunks + LAG, last_steps, 0)
     for b in range(blocks):
         block_store(7 + b, gin_ref, gin_hbm, b).wait()
         block_store(7 + blocks + b, out_ref, out_hbm, b).wait()

time: 112 us -> 108 us (0.964)
  Pallas kernels: 111 us -> 107 us
    pallas_call x1, Pallas kernels: 107 us -> 104 us  [fused_layer(): pl.pallas_call(functools.partial(layer_kernel, shards), out_shape=out_sha...]
where the time goes in v4:
time: 108 us
  Pallas kernels  107 us (99%)
    pallas_call x1, Pallas kernels, fused_layer(): pl.pallas_call(functools.partial(layer_kernel, shards), out_shape=out_sha...  104 us
    pallas_call x1, Pallas kernels, publish(): pl.pallas_call(functools.partial(publish_kernel, count), out_shape=[jax.S...  3.33 us

profile of v4, /device:TPU:0, one launch (start us, length us, event | category | flops | bytes accessed | tf_op | source)
XLA Modules:
  0.0 107.8 jit_solution(11673492622036630619)
XLA Ops:
  0.6 103.6 %layer.1 = (bf16[512,768]{1,0:T(8,128)(2,1)}, f32[512,768]{1,0:T(8,128)}, f32[96,192]{1,0:T(8,128)}, f32[96,192]{1,0:T(8,128)}, f32[96,192]{1,0:T(8,128)}, /*ind...) custom-call(bf16[512,768]{1,0:T(8,128)(2,1)} %bitcast.10, ...), custom_call_target="tpu_custom_call" | custom-call | tf_op jit(solution)/shard_map/layer/pallas_call | solution.py:1480
  104.3 3.3 %publish.1 = (bf16[512,768]{1,0:T(8,128)(2,1)}, f32[512,768]{1,0:T(8,128)}, f32[96,192]{1,0:T(8,128)}, f32[96,192]{1,0:T(8,128)}, f32[96,192]{1,0:T(8,128)}, /*i...) custom-call(bf16[512,768]{1,0:T(8,128)(2,1)} %get-tuple-element.36.r, ...), custom_call_target="tpu_custom_call" | custom-call | tf_op jit(solution)/shard_map/publish/pallas_call | solution.py:1517

commit v5 on v4

--- a/solution.py
+++ b/solution.py
@@ -765,7 +765,6 @@
     kv_copies[1].start()
     gather_corner(1)
     lax.fori_loop(key_blocks * 3 // 4, key_blocks, bias_rows, 0)
-    n1t[...] = normed.T
     gather_pass(2)
     for k in range(1, 4):
         out_copies[k - 1].wait_recv()
@@ -888,6 +887,7 @@
     relays(early, 2)
     gather_corner(4)
     k_t[...] = k_all[...].T
+    n1t[...] = n1[...].T
     dk[...] = jnp.zeros_like(dk)
     dv[...] = jnp.zeros_like(dv)
     small[...] = jnp.zeros_like(small)
@@ -912,6 +912,11 @@
         up = contract(normed, weight(wf, 1), 1, 0)
         down = weight(wf, 2)
         grad_act = contract(cot_ref[at, :], down, 1, 0)
+
+        @pl.when(b > 1)
+        def _():
+            serve((b - 2) * per_block + per_block // 2, per_block // 2)
+
         square = gate * gate
         curve = jnp.tanh(scale * (gate + 0.044715 * square * gate))
         left = 0.5 * (1.0 + curve)
@@ -931,11 +936,12 @@
 
         @pl.when(b > 0)
         def _():
-            serve((b - 1) * per_block, per_block)
+            serve((b - 1) * per_block, per_block // 2)
 
         return carry
 
     lax.fori_loop(0, blocks, feed_forward, 0)
+    serve((blocks - 2) * per_block + per_block // 2, per_block // 2)
 
     def put_outputs(b, carry):
         put_block(1, b)
@@ -1171,20 +1177,13 @@
         store_grad(gsa, i, 2, contract(part_rows, dq_t[...], 1, 1))
         return carry
 
-    lax.fori_loop(0, groups, weights_back, 0)
-    over_copy(2).start()
     serve(step, 2 * chunks - step)
     step = 2 * chunks
-    turned[0] = grl[...].T
 
     def output_weights(i, carry):
         store_grad(gsa, i, 3, contract(turned[0, pair_rows(i), :], att_all[own_rows, :], 1, 1))
         return carry
 
-    lax.fori_loop(0, groups, output_weights, 0)
-    over_copy(1).start()
-    reduce_send(2)
-    reduce_send(1)
 
     def bucket_sums(h, carry):
         for b in range(2 * half):
@@ -1312,26 +1311,55 @@
     def last_steps(n, carry):
         service(2 * chunks + n)
 
-        @pl.when(jnp.logical_and(inner, jnp.logical_and(lax.rem(n, 2) == 0, n < 2 * heads)))
+        @pl.when(n < groups)
         def _():
-            bucket_sums(lax.div(n, 2), 0)
-
-        pl.when(jnp.logical_and(inner, n == 2 * heads))(far_sums)
-        at_step(n, 2 * heads + 1, small_start)
-        at_step(n, 2 * heads + 2, functools.partial(reduce_finish, 0))
-
-        @pl.when(jnp.logical_and(n > 2 * heads + 2, n <= 2 * heads + 2 + blocks))
+            weights_back(n, 0)
+
+        def turn():
+            over_copy(2).start()
+            turned[0] = grl[...].T
+
+        at_step(n, groups - 1, turn)
+
+        @pl.when(jnp.logical_and(n >= groups, n < 2 * groups))
         def _():
-            layer_out(n - 2 * heads - 3)
+            output_weights(n - groups, 0)
+
+        at_step(n, groups + 1, functools.partial(reduce_send, 2))
+        at_step(n, 2 * groups - 1, over_copy(1).start)
+        at_step(n, 2 * groups + 1, functools.partial(reduce_send, 1))
+        after = n - 2 * groups
+
+        @pl.when(
+            jnp.logical_and(
+                jnp.logical_and(inner, lax.rem(n, 2) == 0),
+                jnp.logical_and(after >= 0, after < 2 * heads),
+            )
+        )
+        def _():
+            bucket_sums(lax.div(after, 2), 0)
+
+        def sums_out():
+            pl.when(inner)(far_sums)
+            small_start()
+
+        at_step(n, 2 * groups + 2 * heads - 1, sums_out)
+        for due_step, b in zip((6, 9, 13, 14), range(blocks)):
+
+            @pl.when(n == due_step)
+            def _(b=b):
+                layer_out(b)
+
+        at_step(n, chunks - 2, functools.partial(reduce_finish, 0))
 
         def gains():
             reduce_finish(2)
             gain_start()
 
-        at_step(n, 2 * heads + 3 + blocks, gains)
-        at_step(n, 2 * heads + 4 + blocks, small_finish)
-        at_step(n, 2 * heads + 5 + blocks, functools.partial(reduce_finish, 1))
-        at_step(n, chunks + LAG - 2, gain_finish)
+        at_step(n, chunks, gains)
+        at_step(n, chunks + 1, small_finish)
+        at_step(n, chunks + 2, functools.partial(reduce_finish, 1))
+        at_step(n, chunks + 3, gain_finish)
 
         due = n - (per_block - 1) - LAG
 

time: 108 us -> 107 us (level)
    pallas_call x1, Pallas kernels: 104 us -> 102 us  [fused_layer(): pl.pallas_call(functools.partial(layer_kernel, shards), out_shape=out_sha...]
where the time goes in v5:
time: 107 us
  Pallas kernels  106 us (99%)
    pallas_call x1, Pallas kernels, fused_layer(): pl.pallas_call(functools.partial(layer_kernel, shards), out_shape=out_sha...  102 us
    pallas_call x1, Pallas kernels, publish(): pl.pallas_call(functools.partial(publish_kernel, count), out_shape=[jax.S...  3.33 us

profile of v5, /device:TPU:0, one launch (start us, length us, event | category | flops | bytes accessed | tf_op | source)
XLA Modules:
  0.0 106.6 jit_solution(17593378614589636718)
XLA Ops:
  0.6 102.4 %layer.1 = (bf16[512,768]{1,0:T(8,128)(2,1)}, f32[512,768]{1,0:T(8,128)}, f32[96,192]{1,0:T(8,128)}, f32[96,192]{1,0:T(8,128)}, f32[96,192]{1,0:T(8,128)}, /*ind...) custom-call(bf16[512,768]{1,0:T(8,128)(2,1)} %bitcast.10, ...), custom_call_target="tpu_custom_call" | custom-call | tf_op jit(solution)/shard_map/layer/pallas_call | solution.py:1508
  103.1 3.3 %publish.1 = (bf16[512,768]{1,0:T(8,128)(2,1)}, f32[512,768]{1,0:T(8,128)}, f32[96,192]{1,0:T(8,128)}, f32[96,192]{1,0:T(8,128)}, f32[96,192]{1,0:T(8,128)}, /*i...) custom-call(bf16[512,768]{1,0:T(8,128)(2,1)} %get-tuple-element.36.r, ...), custom_call_target="tpu_custom_call" | custom-call | tf_op jit(solution)/shard_map/publish/pallas_call | solution.py:1545

commit v6 on v5

--- a/solution.py
+++ b/solution.py
@@ -309,7 +309,7 @@
 LAG = 4
 RELAY_ROWS = 32
 EARLY = 4
-PACES = (1, 1, 1)
+PACES = (1, 2, 1)
 
 
 def contract(left, right, left_dim, right_dim, precision=None):
@@ -1359,7 +1359,6 @@
         at_step(n, chunks, gains)
         at_step(n, chunks + 1, small_finish)
         at_step(n, chunks + 2, functools.partial(reduce_finish, 1))
-        at_step(n, chunks + 3, gain_finish)
 
         due = n - (per_block - 1) - LAG
 
@@ -1370,6 +1369,7 @@
         return carry
 
     lax.fori_loop(0, chunks + LAG, last_steps, 0)
+    gain_finish()
     for b in range(blocks):
         block_store(7 + b, gin_ref, gin_hbm, b).wait()
         block_store(7 + blocks + b, out_ref, out_hbm, b).wait()

time: 107 us -> 106 us (level)
  no operation moved by 1% of the time
where the time goes in v6:
time: 106 us
  Pallas kernels  105 us (99%)
    pallas_call x1, Pallas kernels, fused_layer(): pl.pallas_call(functools.partial(layer_kernel, shards), out_shape=out_sha...  102 us
    pallas_call x1, Pallas kernels, publish(): pl.pallas_call(functools.partial(publish_kernel, count), out_shape=[jax.S...  3.33 us

profile of v6, /device:TPU:0, one launch (start us, length us, event | category | flops | bytes accessed | tf_op | source)
XLA Modules:
  0.0 106.2 jit_solution(4594788725898454378)
XLA Ops:
  0.6 102.1 %layer.1 = (bf16[512,768]{1,0:T(8,128)(2,1)}, f32[512,768]{1,0:T(8,128)}, f32[96,192]{1,0:T(8,128)}, f32[96,192]{1,0:T(8,128)}, f32[96,192]{1,0:T(8,128)}, /*ind...) custom-call(bf16[512,768]{1,0:T(8,128)(2,1)} %bitcast.10, ...), custom_call_target="tpu_custom_call" | custom-call | tf_op jit(solution)/shard_map/layer/pallas_call | solution.py:1508
  102.7 3.3 %publish.1 = (bf16[512,768]{1,0:T(8,128)(2,1)}, f32[512,768]{1,0:T(8,128)}, f32[96,192]{1,0:T(8,128)}, f32[96,192]{1,0:T(8,128)}, f32[96,192]{1,0:T(8,128)}, /*i...) custom-call(bf16[512,768]{1,0:T(8,128)(2,1)} %get-tuple-element.36.r, ...), custom_call_target="tpu_custom_call" | custom-call | tf_op jit(solution)/shard_map/publish/pallas_call | solution.py:1545

commit v7 on v6

--- a/solution.py
+++ b/solution.py
@@ -1356,7 +1356,7 @@
             reduce_finish(2)
             gain_start()
 
-        at_step(n, chunks, gains)
+        at_step(n, chunks - 1, gains)
         at_step(n, chunks + 1, small_finish)
         at_step(n, chunks + 2, functools.partial(reduce_finish, 1))
 

time: 106 us -> 106 us (level)
  no operation moved by 1% of the time
where the time goes in v7:
time: 106 us
  Pallas kernels  105 us (99%)
    pallas_call x1, Pallas kernels, fused_layer(): pl.pallas_call(functools.partial(layer_kernel, shards), out_shape=out_sha...  102 us
    pallas_call x1, Pallas kernels, publish(): pl.pallas_call(functools.partial(publish_kernel, count), out_shape=[jax.S...  3.33 us

profile of v7, /device:TPU:0, one launch (start us, length us, event | category | flops | bytes accessed | tf_op | source)
XLA Modules:
  0.0 106.2 jit_solution(7102514828801456097)
XLA Ops:
  0.6 102.1 %layer.1 = (bf16[512,768]{1,0:T(8,128)(2,1)}, f32[512,768]{1,0:T(8,128)}, f32[96,192]{1,0:T(8,128)}, f32[96,192]{1,0:T(8,128)}, f32[96,192]{1,0:T(8,128)}, /*ind...) custom-call(bf16[512,768]{1,0:T(8,128)(2,1)} %bitcast.10, ...), custom_call_target="tpu_custom_call" | custom-call | tf_op jit(solution)/shard_map/layer/pallas_call | solution.py:1508
  102.7 3.3 %publish.1 = (bf16[512,768]{1,0:T(8,128)(2,1)}, f32[512,768]{1,0:T(8,128)}, f32[96,192]{1,0:T(8,128)}, f32[96,192]{1,0:T(8,128)}, f32[96,192]{1,0:T(8,128)}, /*i...) custom-call(bf16[512,768]{1,0:T(8,128)(2,1)} %get-tuple-element.36.r, ...), custom_call_target="tpu_custom_call" | custom-call | tf_op jit(solution)/shard_map/publish/pallas_call | solution.py:1545
